TPU v7x, 1024 devices: a whole 4x8x16 slice. The times are simulated.
1024 devices in a mesh: lon: 64 (over z, y_hi, core), lat: 4 (over y_lo), segment: 4 (over x).
Axes of the slice: x: 4, y: 8 (y_hi: 2, y_lo: 4; y = y_hi * 4 + y_lo), z: 16, core: 2. Of those that a mesh axis runs over, the one named last changes fastest.
Arguments:
- inputs: bfloat16 [2, 64, 256, 512], P(None, 'lat', 'lon'), may hold values from -6 to 6
- cotangent: bfloat16 [2, 64, 256, 512], P(None, 'lat', 'lon'), may hold values from -6 to 6
- weights: bfloat16 [4, 3, 512, 512], P('segment'), may hold values from -0.15625 to 0.15625
- basis_values: float32 [64, 9, 3], replicated, may hold values from 0.05 to 0.5
- lat_step: int32 [64, 9], replicated, may hold values from -2 to 2, as said below
- lon_step: int32 [64, 9], replicated, may hold values from -2 to 2, as said below
Outputs:
- section_out: bfloat16 [4, 2, 64, 256, 512], P('segment', None, 'lat', 'lon')
- section_grad: bfloat16 [4, 2, 64, 256, 512], P('segment', None, 'lat', 'lon')
- weight_grad: float32 [4, 786432], P('segment', ('lon', 'lat'))
Inputs may be any that keep to these rules, and one draw needn't show every extreme that they name: `lat_step`: row offsets of the support points; 2 and -2 each occur. `lon_step`: column offsets of the support points; 2 and -2 each occur.
All inputs are finite; a program needn't handle non-finite values.
Results may differ from a plain program's by a relative error of at most 0.017.
Values may be sent and summed in bfloat16 or wider, within the bound.
A program may use at most 32 MiB of HBM per device.

v0:
```python
import math

import jax
import jax.numpy as jnp
from jax import lax
from jax.sharding import PartitionSpec as P

BASIS = 3
TAPS = 9
REACH = 2


def with_halo(array, sides, width):
    for axis, dim in sides:
        size, length = (lax.axis_size(axis), array.shape[dim])
        up = [(i, (i + 1) % size) for i in range(size)]
        down = [(j, i) for i, j in up]
        last = lax.slice_in_dim(array, length - width, length, axis=dim)
        first = lax.slice_in_dim(array, 0, width, axis=dim)
        before = lax.ppermute(last, axis, up)
        after = lax.ppermute(first, axis, down)
        array = jnp.concatenate([before, array, after], axis=dim)
    return array


def shifted(block, axis, distance):
    devices = range(lax.axis_size(axis))
    route = [(i - distance, i) for i in devices if i - distance in devices]
    return lax.ppermute(block, axis, route)


def widen(features):
    return with_halo(features, (("lon", 2), ("lat", 1)), REACH)


def pass_ahead(result):
    return shifted(result, "segment", 1)


def pass_behind(result):
    return shifted(result, "segment", -1)


def build_tables(basis_values, lat_step, lon_step, lat_rows, lon_cols, lat_index, lat_total):
    pad_rows = lat_rows + 2 * REACH
    pad_cols = lon_cols + 2 * REACH
    lat_padded = jnp.pad(lat_step, ((REACH, REACH), (0, 0)))
    lon_padded = jnp.pad(lon_step, ((REACH, REACH), (0, 0)))
    basis_padded = jnp.pad(basis_values, ((REACH, REACH), (0, 0), (0, 0)))
    row_start = lat_index * lat_rows
    lat_near = lax.dynamic_slice_in_dim(lat_padded, row_start, pad_rows, 0)
    lon_near = lax.dynamic_slice_in_dim(lon_padded, row_start, pad_rows, 0)
    basis_near = lax.dynamic_slice_in_dim(basis_padded, row_start, pad_rows, 0)
    lat_own = lat_near[REACH : REACH + lat_rows]
    lon_own = lon_near[REACH : REACH + lat_rows]
    basis_own = basis_near[REACH : REACH + lat_rows]
    own_rows = row_start + jnp.arange(lat_rows)
    inside = (own_rows[:, None] + lat_own >= 0) & (own_rows[:, None] + lat_own < lat_total)
    row_grid = jnp.arange(lat_rows)[:, None, None]
    col_grid = jnp.arange(lon_cols)[None, :, None]
    source = (row_grid + REACH + lat_own[:, None, :]) * pad_cols + (
        col_grid + REACH + lon_own[:, None, :]
    )
    tap_weight = jnp.where(inside[:, None, :, None], basis_own[:, None, :, :], 0.0)
    tap_weight = jnp.broadcast_to(tap_weight, (lat_rows, lon_cols, TAPS, BASIS))
    picker = (source[..., None] == jnp.arange(pad_rows * pad_cols)).astype(jnp.float32)
    forward_map = jnp.einsum("ijkb,ijks->bijs", tap_weight, picker, precision=lax.Precision.HIGHEST)
    forward_map = forward_map.reshape(BASIS, lat_rows * lon_cols, pad_rows * pad_cols)
    near_rows = row_start - REACH + jnp.arange(pad_rows)
    real_row = (near_rows >= 0) & (near_rows < lat_total)
    pad_row_grid = jnp.arange(pad_rows)[:, None, None]
    pad_col_grid = jnp.arange(pad_cols)[None, :, None]
    target_row = pad_row_grid - REACH + lat_near[:, None, :]
    target_col = pad_col_grid - REACH + lon_near[:, None, :]
    landed = (
        (target_row >= 0)
        & (target_row < lat_rows)
        & (target_col >= 0)
        & (target_col < lon_cols)
        & real_row[:, None, None]
    )
    target = target_row * lon_cols + target_col
    back_weight = jnp.where(landed[..., None], basis_near[:, None, :, :], 0.0)
    catcher = (target[..., None] == jnp.arange(lat_rows * lon_cols)).astype(jnp.float32)
    backward_map = jnp.einsum(
        "pqkb,pqkt->btpq", back_weight, catcher, precision=lax.Precision.HIGHEST
    )
    backward_map = backward_map.reshape(BASIS, lat_rows * lon_cols, pad_rows * pad_cols)
    return (forward_map, backward_map)


def per_device(inputs, cotangent, weights, basis_values, lat_step, lon_step):
    members, lat_rows, lon_cols, channels = inputs.shape
    pad_rows = lat_rows + 2 * REACH
    pad_cols = lon_cols + 2 * REACH
    cells = lat_rows * lon_cols
    lat_index = lax.axis_index("lat")
    lat_total = lat_rows * lax.axis_size("lat")
    segment_index = lax.axis_index("segment")
    depth = lax.axis_size("segment")
    grad_scale = 1.0 / math.sqrt(members * lat_total * lon_cols * lax.axis_size("lon"))
    forward_map, backward_map = build_tables(
        basis_values, lat_step, lon_step, lat_rows, lon_cols, lat_index, lat_total
    )
    kernel = weights[0]
    keep_spread = jnp.zeros((BASIS, members, cells, channels), jnp.bfloat16)
    keep_mixed = jnp.zeros((members, cells, channels), jnp.float32)
    keep_gate = jnp.zeros((members, cells, channels), jnp.bfloat16)
    section_out = jnp.zeros(inputs.shape, jnp.bfloat16)
    section_grad = jnp.zeros(inputs.shape, jnp.bfloat16)
    carry = inputs
    for tick_num in range(depth):
        layer_count = carry.shape[0]
        layer_padded = (
            widen(carry).reshape(layer_count, pad_rows * pad_cols, channels).astype(jnp.float32)
        )
        spread = jnp.einsum(
            "bts,msc->bmtc", forward_map, layer_padded, precision=lax.Precision.HIGHEST
        ).astype(jnp.bfloat16)
        layer_mixed = jnp.einsum(
            "bmtc,bcd->mtd", spread, kernel, preferred_element_type=jnp.float32
        )
        result = (
            carry.reshape(layer_count, cells, channels).astype(jnp.float32)
            + jax.nn.silu(layer_mixed)
        ).astype(jnp.bfloat16)
        spread, mixed, result = (spread, layer_mixed, result.reshape(carry.shape))
        here = segment_index == tick_num
        keep_spread = jnp.where(here, spread, keep_spread)
        keep_mixed = jnp.where(here, mixed, keep_mixed)
        section_out = jnp.where(here, result, section_out)
        if tick_num + 1 < depth:
            carry = pass_ahead(result)
    grad = cotangent
    for tick_num in range(depth):
        count = grad.shape[0]
        flat_grad = grad.reshape(count, cells, channels).astype(jnp.float32)
        sigma = jax.nn.sigmoid(keep_mixed)
        gate_grad = (flat_grad * sigma * (1.0 + keep_mixed * (1.0 - sigma))).astype(jnp.bfloat16)
        feature_grad = jnp.einsum(
            "mtd,bcd->bmtc", gate_grad, kernel, preferred_element_type=jnp.float32
        ).astype(jnp.bfloat16)
        padded = widen(feature_grad.reshape(BASIS * count, lat_rows, lon_cols, channels))
        padded = padded.reshape(BASIS, count, pad_rows * pad_cols, channels).astype(jnp.float32)
        pulled = jnp.einsum("bts,bmsc->mtc", backward_map, padded, precision=lax.Precision.HIGHEST)
        new_grad = (flat_grad + pulled).astype(jnp.bfloat16).reshape(grad.shape)
        gate_grad, new_grad = (gate_grad, new_grad)
        here = segment_index == depth - 1 - tick_num
        keep_gate = jnp.where(here, gate_grad, keep_gate)
        section_grad = jnp.where(here, new_grad, section_grad)
        if tick_num + 1 < depth:
            grad = pass_behind(new_grad)
    local_grad = (
        jnp.einsum("bmtc,mtd->bcd", keep_spread, keep_gate, preferred_element_type=jnp.float32)
        * grad_scale
    )
    owners = lax.axis_size("lon") * lax.axis_size("lat")
    grad_rows = local_grad.reshape(owners, -1)
    weight_grad = lax.psum_scatter(grad_rows, ("lon", "lat"), scatter_dimension=0, tiled=True)
    return (section_out[None], section_grad[None], weight_grad)


def solution(mesh):
    return jax.shard_map(
        per_device,
        mesh=mesh,
        in_specs=(
            P(None, "lat", "lon", None),
            P(None, "lat", "lon", None),
            P("segment", None, None, None),
            P(),
            P(),
            P(),
        ),
        out_specs=(
            P("segment", None, "lat", "lon", None),
            P("segment", None, "lat", "lon", None),
            P("segment", ("lon", "lat")),
        ),
        check_vma=False,
    )
```

profile of v0, /device:TPU:1, one launch (start us, length us, event | category | flops | bytes accessed | tf_op | source)
XLA Modules:
  0.0 639.5 jit_solution(6400850332140399421)
XLA Ops:
  8.4 16.1 %collective-permute-start.1 = (bf16[2,16,2,512]{3,2,1,0:T(2,128)(2,1)S(1)}, bf16[2,16,2,512]{3,2,1,0:T(2,128)(2,1)S(1)}, u32[]{:S(2)}, u32[]{:S(2)}) collective-permute-start(bf16[2,16,2,512]{3,2,1,0:T(2,128)(2,1)S(1)} %get-tuple-element.36), channel_id=1, source_target_pairs={{16,0},{32,16},{48,32},{64,48},{80,64},{96,80},{112,96},{128,112},... | collective-permute-start | bytes 196616 | tf_op jit(solution)/shard_map/ppermute | solution.py:21
  24.5 1.9 collective-permute-start
  29.2 6.3 collective-permute-done
  36.3 2.5 collective-permute-start.3
  38.9 2.7 collective-permute-start.2
  43.2 2.1 collective-permute-done.2
  47.9 3.1 collective-permute-start.4
  51.0 1.9 collective-permute-done.4
  53.0 13.6 %collective-permute-start.6 = (bf16[2,16,2,512]{3,2,1,0:T(2,128)(2,1)S(1)}, bf16[2,16,2,512]{3,2,1,0:T(2,128)(2,1)S(1)}, u32[]{:S(2)}, u32[]{:S(2)}) collective-permute-start(bf16[2,16,2,512]{3,2,1,0:T(2,128)(2,1)S(1)} %get-tuple-element.34), channel_id=1, source_target_pairs={{16,0},{32,16},{48,32},{64,48},{80,64},{96,80},{112,96},{128,112},... | collective-permute-start | bytes 196616 | tf_op jit(solution)/shard_map/ppermute | solution.py:21
  66.7 1.9 collective-permute-start.5
  70.0 1.9 collective-permute-start.8
  71.9 3.4 collective-permute-start.7
  75.3 3.0 collective-permute-done.7
  80.9 4.1 collective-permute-start.9
  87.0 12.3 %collective-permute-start.11 = (bf16[2,16,2,512]{3,2,1,0:T(2,128)(2,1)S(1)}, bf16[2,16,2,512]{3,2,1,0:T(2,128)(2,1)S(1)}, u32[]{:S(2)}, u32[]{:S(2)}) collective-permute-start(bf16[2,16,2,512]{3,2,1,0:T(2,128)(2,1)S(1)} %get-tuple-element.32), channel_id=1, source_target_pairs={{16,0},{32,16},{48,32},{64,48},{80,64},{96,80},{112,96},{128,112},... | collective-permute-start | bytes 196616 | tf_op jit(solution)/shard_map/ppermute | solution.py:21
  99.3 1.9 collective-permute-start.10
  102.6 1.9 collective-permute-start.13
  104.5 3.4 collective-permute-start.12
  108.6 2.4 collective-permute-done.12
  114.6 4.1 collective-permute-start.14
  120.7 12.3 %collective-permute-start.16 = (bf16[2,16,2,512]{3,2,1,0:T(2,128)(2,1)S(1)}, bf16[2,16,2,512]{3,2,1,0:T(2,128)(2,1)S(1)}, u32[]{:S(2)}, u32[]{:S(2)}) collective-permute-start(bf16[2,16,2,512]{3,2,1,0:T(2,128)(2,1)S(1)} %get-tuple-element.30), channel_id=1, source_target_pairs={{16,0},{32,16},{48,32},{64,48},{80,64},{96,80},{112,96},{128,112},... | collective-permute-start | bytes 196616 | tf_op jit(solution)/shard_map/ppermute | solution.py:21
  133.0 1.9 collective-permute-start.15
  136.3 1.9 collective-permute-start.18
  138.2 3.4 collective-permute-start.17
  141.9 2.8 collective-permute-done.17
  148.5 15.0 %collective-permute-start.20 = (bf16[6,16,2,512]{3,2,1,0:T(2,128)(2,1)S(1)}, bf16[6,16,2,512]{3,2,1,0:T(2,128)(2,1)S(1)}, u32[]{:S(2)}, u32[]{:S(2)}) collective-permute-start(bf16[6,16,2,512]{3,2,1,0:T(2,128)(2,1)S(1)} %get-tuple-element.20), channel_id=1, source_target_pairs={{16,0},{32,16},{48,32},{64,48},{80,64},{96,80},{112,96},{128,112},... | collective-permute-start | bytes 589832 | tf_op jit(solution)/shard_map/ppermute | solution.py:21
  165.6 3.9 collective-permute-done.19
  172.2 3.4 collective-permute-start.21
  175.6 2.7 fusion.16
  183.4 5.1 collective-permute-done.23
  189.8 11.0 %collective-permute-start.25 = (bf16[6,16,2,512]{3,2,1,0:T(2,128)(2,1)S(1)}, bf16[6,16,2,512]{3,2,1,0:T(2,128)(2,1)S(1)}, u32[]{:S(2)}, u32[]{:S(2)}) collective-permute-start(bf16[6,16,2,512]{3,2,1,0:T(2,128)(2,1)S(1)} %get-tuple-element.18), channel_id=1, source_target_pairs={{16,0},{32,16},{48,32},{64,48},{80,64},{96,80},{112,96},{128,112},... | collective-permute-start | bytes 589832 | tf_op jit(solution)/shard_map/ppermute | solution.py:21
  200.8 1.9 collective-permute-start.24
  205.4 3.6 collective-permute-start.27
  209.0 2.5 collective-permute-start.26
  211.7 4.5 collective-permute-done.26
  218.9 4.7 collective-permute-done.28
  224.9 13.1 %collective-permute-start.30 = (bf16[6,16,2,512]{3,2,1,0:T(2,128)(2,1)S(1)}, bf16[6,16,2,512]{3,2,1,0:T(2,128)(2,1)S(1)}, u32[]{:S(2)}, u32[]{:S(2)}) collective-permute-start(bf16[6,16,2,512]{3,2,1,0:T(2,128)(2,1)S(1)} %get-tuple-element.16), channel_id=1, source_target_pairs={{16,0},{32,16},{48,32},{64,48},{80,64},{96,80},{112,96},{128,112},... | collective-permute-start | bytes 589832 | tf_op jit(solution)/shard_map/ppermute | solution.py:21
  239.9 2.6 collective-permute-done.29
  244.6 3.5 collective-permute-start.31
  248.3 3.6 collective-permute-done.31
  254.6 4.7 collective-permute-done.33
  259.5 3.3 bitcast_multiply_fusion
  262.8 5.1 reshape.275
  269.8 13.1 %collective-permute-start.35 = (bf16[6,16,2,512]{3,2,1,0:T(2,128)(2,1)}, bf16[6,16,2,512]{3,2,1,0:T(2,128)(2,1)S(1)}, u32[]{:S(2)}, u32[]{:S(2)}) collective-permute-start(bf16[6,16,2,512]{3,2,1,0:T(2,128)(2,1)} %get-tuple-element.14), channel_id=1, source_target_pairs={{16,0},{32,16},{48,32},{64,48},{80,64},{96,80},{112,96},{128,112},... | collective-permute-start | bytes 589832 | tf_op jit(solution)/shard_map/ppermute | solution.py:21
  283.0 1.9 collective-permute-start.34
  291.3 3.8 collective-permute-start.36
  301.9 328.6 %all-reduce.6.cloned.1.call-done = f32[256,3072]{1,0:T(8,128)} async-done(((f32[256,3072]{1,0:T(8,128)}), f32[256,3072]{1,0:T(8,128)}) %all-reduce.6.cloned.1.call-update) | async-done | bytes 3145744
  630.5 2.1 constant_dynamic-slice_fusion
  (178 shorter events, 68.0 us)
Async XLA Ops:
  7.2 39.6 %copy-start = (bf16[1,3,512,512]{3,2,1,0:T(8,128)(2,1)S(1)}, bf16[1,3,512,512]{3,2,1,0:T(8,128)(2,1)}, u32[]{:S(2)}) copy-start(bf16[1,3,512,512]{3,2,1,0:T(8,128)(2,1)} %param.8) | copy-start | bytes 4718596
  7.2 38.2 %copy-start.12 = (bf16[2,16,4,512]{3,2,1,0:T(4,128)(2,1)S(1)}, bf16[2,16,4,512]{3,2,1,0:T(4,128)(2,1)}, u32[]{:S(2)}) copy-start(bf16[2,16,4,512]{3,2,1,0:T(4,128)(2,1)} %param.6) | copy-start | bytes 393220
  7.2 623.3 %all-reduce.6.cloned.1.call-start = ((), (), s32[]{:S(2)}) async-start(), calls=%async_computation | async-start | bytes 6291456
  8.4 20.8 %collective-permute-start.1 = (bf16[2,16,2,512]{3,2,1,0:T(2,128)(2,1)S(1)}, bf16[2,16,2,512]{3,2,1,0:T(2,128)(2,1)S(1)}, u32[]{:S(2)}, u32[]{:S(2)}) collective-permute-start(bf16[2,16,2,512]{3,2,1,0:T(2,128)(2,1)S(1)} %get-tuple-element.36), channel_id=1, source_target_pairs={{16,0},{32,16},{48,32},{64,48},{80,64},{96,80},{112,96},{128,112},... | collective-permute-start | bytes 196616 | tf_op jit(solution)/shard_map/ppermute | solution.py:21
  24.5 11.0 %collective-permute-start = (bf16[2,16,2,512]{3,2,1,0:T(2,128)(2,1)S(1)}, bf16[2,16,2,512]{3,2,1,0:T(2,128)(2,1)S(1)}, u32[]{:S(2)}, u32[]{:S(2)}) collective-permute-start(bf16[2,16,2,512]{3,2,1,0:T(2,128)(2,1)S(1)} %get-tuple-element.35), channel_id=1, source_target_pairs={{0,16},{16,32},{32,48},{48,64},{64,80},{80,96},{96,112},{112,128},... | collective-permute-start | bytes 196616 | tf_op jit(solution)/shard_map/ppermute | solution.py:20
  36.3 6.9 %collective-permute-start.3 = (bf16[2,2,8,512]{3,2,1,0:T(8,128)(2,1)S(1)}, bf16[2,2,8,512]{3,2,1,0:T(8,128)(2,1)S(1)}, u32[]{:S(2)}, u32[]{:S(2)}) collective-permute-start(bf16[2,2,8,512]{3,2,1,0:T(8,128)(2,1)S(1)} %get-tuple-element.28), channel_id=1, source_target_pairs={{4,0},{8,4},{12,8},{0,12},{5,1},{9,5},{13,9},{1,13},{6,2},{10,6},{... | collective-permute-start | bytes 98312 | tf_op jit(solution)/shard_map/ppermute | solution.py:21
  38.9 6.5 %collective-permute-start.2 = (bf16[2,2,8,512]{3,2,1,0:T(8,128)(2,1)S(1)}, bf16[2,2,8,512]{3,2,1,0:T(8,128)(2,1)S(1)}, u32[]{:S(2)}, u32[]{:S(2)}) collective-permute-start(bf16[2,2,8,512]{3,2,1,0:T(8,128)(2,1)S(1)} %get-tuple-element.27), channel_id=1, source_target_pairs={{0,4},{4,8},{8,12},{12,0},{1,5},{5,9},{9,13},{13,1},{2,6},{6,10},{... | collective-permute-start | bytes 98312 | tf_op jit(solution)/shard_map/ppermute | solution.py:20
  42.2 68.8 %copy-start.25 = (f32[16,4,160,3]{2,3,1,0:T(4,128)}, f32[16,4,160,3]{2,3,1,0:T(4,128)S(1)}, u32[]{:S(2)}) copy-start(f32[16,4,160,3]{2,3,1,0:T(4,128)S(1)} %fusion.66) | copy-start | bytes 368644
  47.9 5.1 collective-permute-start.4
  53.0 15.6 %collective-permute-start.6 = (bf16[2,16,2,512]{3,2,1,0:T(2,128)(2,1)S(1)}, bf16[2,16,2,512]{3,2,1,0:T(2,128)(2,1)S(1)}, u32[]{:S(2)}, u32[]{:S(2)}) collective-permute-start(bf16[2,16,2,512]{3,2,1,0:T(2,128)(2,1)S(1)} %get-tuple-element.34), channel_id=1, source_target_pairs={{16,0},{32,16},{48,32},{64,48},{80,64},{96,80},{112,96},{128,112},... | collective-permute-start | bytes 196616 | tf_op jit(solution)/shard_map/ppermute | solution.py:21
  66.7 3.2 collective-permute-start.5
  70.0 5.3 collective-permute-start.8
  71.9 6.5 %collective-permute-start.7 = (bf16[2,2,8,512]{3,2,1,0:T(8,128)(2,1)S(1)}, bf16[2,2,8,512]{3,2,1,0:T(8,128)(2,1)S(1)}, u32[]{:S(2)}, u32[]{:S(2)}) collective-permute-start(bf16[2,2,8,512]{3,2,1,0:T(8,128)(2,1)S(1)} %get-tuple-element.25), channel_id=1, source_target_pairs={{0,4},{4,8},{8,12},{12,0},{1,5},{5,9},{9,13},{13,1},{2,6},{6,10},{... | collective-permute-start | bytes 98312 | tf_op jit(solution)/shard_map/ppermute | solution.py:20
  80.9 6.0 collective-permute-start.9
  87.0 14.2 %collective-permute-start.11 = (bf16[2,16,2,512]{3,2,1,0:T(2,128)(2,1)S(1)}, bf16[2,16,2,512]{3,2,1,0:T(2,128)(2,1)S(1)}, u32[]{:S(2)}, u32[]{:S(2)}) collective-permute-start(bf16[2,16,2,512]{3,2,1,0:T(2,128)(2,1)S(1)} %get-tuple-element.32), channel_id=1, source_target_pairs={{16,0},{32,16},{48,32},{64,48},{80,64},{96,80},{112,96},{128,112},... | collective-permute-start | bytes 196616 | tf_op jit(solution)/shard_map/ppermute | solution.py:21
  99.3 3.2 collective-permute-start.10
  102.6 6.0 collective-permute-start.13
  104.5 6.5 %collective-permute-start.12 = (bf16[2,2,8,512]{3,2,1,0:T(8,128)(2,1)S(1)}, bf16[2,2,8,512]{3,2,1,0:T(8,128)(2,1)S(1)}, u32[]{:S(2)}, u32[]{:S(2)}) collective-permute-start(bf16[2,2,8,512]{3,2,1,0:T(8,128)(2,1)S(1)} %get-tuple-element.23), channel_id=1, source_target_pairs={{0,4},{4,8},{8,12},{12,0},{1,5},{5,9},{9,13},{13,1},{2,6},{6,10},{... | collective-permute-start | bytes 98312 | tf_op jit(solution)/shard_map/ppermute | solution.py:20
  112.4 22.5 %copy-start.23 = (f32[64,9,3]{0,2,1:T(4,128)S(1)}, f32[64,9,3]{0,2,1:T(4,128)}, u32[]{:S(2)}) copy-start(f32[64,9,3]{0,2,1:T(4,128)} %param.9) | copy-start | bytes 20740
  112.4 29.2 %copy-start.21 = (bf16[2,16,4,512]{3,2,1,0:T(4,128)(2,1)S(1)}, bf16[2,16,4,512]{3,2,1,0:T(4,128)(2,1)}, u32[]{:S(2)}) copy-start(bf16[2,16,4,512]{3,2,1,0:T(4,128)(2,1)} %param.7) | copy-start | bytes 393220
  114.6 6.0 collective-permute-start.14
  120.6 25.7 %copy-start.13 = (bf16[2,16,4,512]{3,2,1,0:T(4,128)(2,1)}, bf16[2,16,4,512]{3,2,1,0:T(4,128)(2,1)S(1)}, u32[]{:S(2)}) copy-start(bf16[2,16,4,512]{3,2,1,0:T(4,128)(2,1)S(1)} %collective-permute-done.14) | copy-start | bytes 393220
  120.7 14.3 %collective-permute-start.16 = (bf16[2,16,2,512]{3,2,1,0:T(2,128)(2,1)S(1)}, bf16[2,16,2,512]{3,2,1,0:T(2,128)(2,1)S(1)}, u32[]{:S(2)}, u32[]{:S(2)}) collective-permute-start(bf16[2,16,2,512]{3,2,1,0:T(2,128)(2,1)S(1)} %get-tuple-element.30), channel_id=1, source_target_pairs={{16,0},{32,16},{48,32},{64,48},{80,64},{96,80},{112,96},{128,112},... | collective-permute-start | bytes 196616 | tf_op jit(solution)/shard_map/ppermute | solution.py:21
  133.0 3.2 collective-permute-start.15
  136.3 5.6 collective-permute-start.18
  138.2 6.5 %collective-permute-start.17 = (bf16[2,2,8,512]{3,2,1,0:T(8,128)(2,1)S(1)}, bf16[2,2,8,512]{3,2,1,0:T(8,128)(2,1)S(1)}, u32[]{:S(2)}, u32[]{:S(2)}) collective-permute-start(bf16[2,2,8,512]{3,2,1,0:T(8,128)(2,1)S(1)} %get-tuple-element.21), channel_id=1, source_target_pairs={{0,4},{4,8},{8,12},{12,0},{1,5},{5,9},{9,13},{13,1},{2,6},{6,10},{... | collective-permute-start | bytes 98312 | tf_op jit(solution)/shard_map/ppermute | solution.py:20
  148.5 17.1 %collective-permute-start.20 = (bf16[6,16,2,512]{3,2,1,0:T(2,128)(2,1)S(1)}, bf16[6,16,2,512]{3,2,1,0:T(2,128)(2,1)S(1)}, u32[]{:S(2)}, u32[]{:S(2)}) collective-permute-start(bf16[6,16,2,512]{3,2,1,0:T(2,128)(2,1)S(1)} %get-tuple-element.20), channel_id=1, source_target_pairs={{16,0},{32,16},{48,32},{64,48},{80,64},{96,80},{112,96},{128,112},... | collective-permute-start | bytes 589832 | tf_op jit(solution)/shard_map/ppermute | solution.py:21
  163.5 5.9 collective-permute-start.19
  170.3 9.1 %collective-permute-start.22 = (bf16[6,2,8,512]{3,2,1,0:T(8,128)(2,1)}, bf16[6,2,8,512]{3,2,1,0:T(8,128)(2,1)}, u32[]{:S(2)}, u32[]{:S(2)}) collective-permute-start(bf16[6,2,8,512]{3,2,1,0:T(8,128)(2,1)} %get-tuple-element.12), channel_id=1, source_target_pairs={{4,0},{8,4},{12,8},{0,12},{5,1},{9,5},{13,9},{1,13},{6,2},{10,6},{... | collective-permute-start | bytes 294920 | tf_op jit(solution)/shard_map/ppermute | solution.py:21
  172.2 7.6 %collective-permute-start.21 = (bf16[6,2,8,512]{3,2,1,0:T(8,128)(2,1)}, bf16[6,2,8,512]{3,2,1,0:T(8,128)(2,1)}, u32[]{:S(2)}, u32[]{:S(2)}) collective-permute-start(bf16[6,2,8,512]{3,2,1,0:T(8,128)(2,1)} %get-tuple-element.11), channel_id=1, source_target_pairs={{0,4},{4,8},{8,12},{12,0},{1,5},{5,9},{9,13},{13,1},{2,6},{6,10},{... | collective-permute-start | bytes 294920 | tf_op jit(solution)/shard_map/ppermute | solution.py:20
  182.1 6.4 collective-permute-start.23
  189.8 13.7 %collective-permute-start.25 = (bf16[6,16,2,512]{3,2,1,0:T(2,128)(2,1)S(1)}, bf16[6,16,2,512]{3,2,1,0:T(2,128)(2,1)S(1)}, u32[]{:S(2)}, u32[]{:S(2)}) collective-permute-start(bf16[6,16,2,512]{3,2,1,0:T(2,128)(2,1)S(1)} %get-tuple-element.18), channel_id=1, source_target_pairs={{16,0},{32,16},{48,32},{64,48},{80,64},{96,80},{112,96},{128,112},... | collective-permute-start | bytes 589832 | tf_op jit(solution)/shard_map/ppermute | solution.py:21
  200.8 4.5 collective-permute-start.24
  205.4 6.2 collective-permute-start.27
  209.0 7.2 %collective-permute-start.26 = (bf16[6,2,8,512]{3,2,1,0:T(8,128)(2,1)S(1)}, bf16[6,2,8,512]{3,2,1,0:T(8,128)(2,1)S(1)}, u32[]{:S(2)}, u32[]{:S(2)}) collective-permute-start(bf16[6,2,8,512]{3,2,1,0:T(8,128)(2,1)S(1)} %get-tuple-element.9), channel_id=1, source_target_pairs={{0,4},{4,8},{8,12},{12,0},{1,5},{5,9},{9,13},{13,1},{2,6},{6,10},{... | collective-permute-start | bytes 294920 | tf_op jit(solution)/shard_map/ppermute | solution.py:20
  217.6 6.0 collective-permute-start.28
  224.9 15.1 %collective-permute-start.30 = (bf16[6,16,2,512]{3,2,1,0:T(2,128)(2,1)S(1)}, bf16[6,16,2,512]{3,2,1,0:T(2,128)(2,1)S(1)}, u32[]{:S(2)}, u32[]{:S(2)}) collective-permute-start(bf16[6,16,2,512]{3,2,1,0:T(2,128)(2,1)S(1)} %get-tuple-element.16), channel_id=1, source_target_pairs={{16,0},{32,16},{48,32},{64,48},{80,64},{96,80},{112,96},{128,112},... | collective-permute-start | bytes 589832 | tf_op jit(solution)/shard_map/ppermute | solution.py:21
  238.0 4.5 collective-permute-start.29
  242.7 5.7 collective-permute-start.32
  244.6 7.3 %collective-permute-start.31 = (bf16[6,2,8,512]{3,2,1,0:T(8,128)(2,1)S(1)}, bf16[6,2,8,512]{3,2,1,0:T(8,128)(2,1)S(1)}, u32[]{:S(2)}, u32[]{:S(2)}) collective-permute-start(bf16[6,2,8,512]{3,2,1,0:T(8,128)(2,1)S(1)} %get-tuple-element.7), channel_id=1, source_target_pairs={{0,4},{4,8},{8,12},{12,0},{1,5},{5,9},{9,13},{13,1},{2,6},{6,10},{... | collective-permute-start | bytes 294920 | tf_op jit(solution)/shard_map/ppermute | solution.py:20
  253.3 6.0 collective-permute-start.33
  267.9 18.3 %copy-start.14 = (bf16[2,16,4,512]{3,2,1,0:T(4,128)(2,1)S(1)}, bf16[2,16,4,512]{3,2,1,0:T(4,128)(2,1)}, u32[]{:S(2)}) copy-start(bf16[2,16,4,512]{3,2,1,0:T(4,128)(2,1)} %copy-done.13) | copy-start | bytes 393220
  268.5 26.6 %copy-start.16 = (bf16[2,64,512]{2,1,0:T(8,128)(2,1)S(1)}, bf16[2,64,512]{2,1,0:T(8,128)(2,1)}, u32[]{:S(2)}) copy-start(bf16[2,64,512]{2,1,0:T(8,128)(2,1)} %copy-done.15) | copy-start | bytes 393220
  268.6 26.6 %copy-start.18 = (bf16[2,64,512]{2,1,0:T(8,128)(2,1)S(1)}, bf16[2,64,512]{2,1,0:T(8,128)(2,1)}, u32[]{:S(2)}) copy-start(bf16[2,64,512]{2,1,0:T(8,128)(2,1)} %copy-done.17) | copy-start | bytes 393220
  269.8 16.4 %collective-permute-start.35 = (bf16[6,16,2,512]{3,2,1,0:T(2,128)(2,1)}, bf16[6,16,2,512]{3,2,1,0:T(2,128)(2,1)S(1)}, u32[]{:S(2)}, u32[]{:S(2)}) collective-permute-start(bf16[6,16,2,512]{3,2,1,0:T(2,128)(2,1)} %get-tuple-element.14), channel_id=1, source_target_pairs={{16,0},{32,16},{48,32},{64,48},{80,64},{96,80},{112,96},{128,112},... | collective-permute-start | bytes 589832 | tf_op jit(solution)/shard_map/ppermute | solution.py:21
  283.0 4.8 collective-permute-start.34
  289.4 9.1 %collective-permute-start.37 = (bf16[6,2,8,512]{3,2,1,0:T(8,128)(2,1)}, bf16[6,2,8,512]{3,2,1,0:T(8,128)(2,1)}, u32[]{:S(2)}, u32[]{:S(2)}) collective-permute-start(bf16[6,2,8,512]{3,2,1,0:T(8,128)(2,1)} %get-tuple-element.6), channel_id=1, source_target_pairs={{4,0},{8,4},{12,8},{0,12},{5,1},{9,5},{13,9},{1,13},{6,2},{10,6},{... | collective-permute-start | bytes 294920 | tf_op jit(solution)/shard_map/ppermute | solution.py:21
  291.3 7.5 %collective-permute-start.36 = (bf16[6,2,8,512]{3,2,1,0:T(8,128)(2,1)}, bf16[6,2,8,512]{3,2,1,0:T(8,128)(2,1)}, u32[]{:S(2)}, u32[]{:S(2)}) collective-permute-start(bf16[6,2,8,512]{3,2,1,0:T(8,128)(2,1)} %get-tuple-element.5), channel_id=1, source_target_pairs={{0,4},{4,8},{8,12},{12,0},{1,5},{5,9},{9,13},{13,1},{2,6},{6,10},{... | collective-permute-start | bytes 294920 | tf_op jit(solution)/shard_map/ppermute | solution.py:20
  (17 other events, 93.8 us)
Sparse Core Ops, SparseCore 0:
  268.0 362.4 all-reduce.5
where the time goes:
time: 643 us; the launch traced here: 639 us
  waiting for transfers between devices  389 us (60%)
  starting transfers between devices  181 us (28%)
  local copies, waits for them, and re-layouts  21.7 us (3%)
  matrix products  19.4 us (3%)
  between operations  15.1 us (2%)
  other arithmetic  14.1 us (2%)
    unnamed x2, waiting for transfers between devices  329 us
    ppermute x16, starting transfers between devices, with_halo(): after = lax.ppermute(first, axis, down)  124 us
    ppermute x16, starting transfers between devices, with_halo(): before = lax.ppermute(last, axis, up)  41.3 us
    ppermute x16, waiting for transfers between devices, with_halo(): before = lax.ppermute(last, axis, up)  38.9 us
    ppermute x6, waiting for transfers between devices, shifted(): return lax.ppermute(block, axis, route)  19.9 us
    ppermute x6, starting transfers between devices, shifted(): return lax.ppermute(block, axis, route)  15.2 us
  transfers between devices with their start and end apart: 39, of which 26 were waited for; matrix products, arithmetic and copies ran while one was open for 3% of the time, Pallas kernels for 0%

commit v1 on v0

v1 whole, which is shorter than its diff:
```python
import functools
import math

import jax
import jax.numpy as jnp
import numpy as np
from jax import lax
from jax.experimental import pallas as pl
from jax.experimental.pallas import tpu as pltpu
from jax.sharding import PartitionSpec as P

BASIS = 3
TAPS = 9
REACH = 2
LANES = 128
MESH = pl.DeviceIdType.MESH
F32 = jnp.float32
BF16 = jnp.bfloat16


def cell_index(row, col, rows, half):
    return (col // half) * (rows * half) + row * half + col % half


def halo_cells(rows, cols):
    cells = []
    for col in (-2, cols):
        cells += [(i, col + j) for i in range(rows) for j in range(2)]
    for row in (-2, rows):
        cells += [(row + i, j) for i in range(2) for j in range(cols)]
    for row in (-2, rows):
        for col in (-2, cols):
            cells += [(row + i, col + j) for i in range(2) for j in range(2)] + [None] * 4
    return cells


def static_tables(rows, cols, half):
    own = rows * cols
    cells = [None] * own
    for i in range(rows):
        for j in range(cols):
            cells[cell_index(i, j, rows, half)] = (i, j)
    halo = halo_cells(rows, cols)
    pick = np.zeros((len(halo), own), np.float32)
    for slot, cell in enumerate(halo):
        if cell is not None:
            pick[slot, cell_index(cell[0] % rows, cell[1] % cols, rows, half)] = 1
    near = rows + 8
    spots = cells + halo
    spot_rows = np.zeros((near, len(spots)), np.float32)
    spot_at = np.full((16, len(spots)), -100, np.int32)
    for s, cell in enumerate(spots):
        if cell is not None:
            spot_rows[cell[0] + REACH, s] = 1
            spot_at[0, s], spot_at[1, s] = cell
    own_rows = np.ascontiguousarray(spot_rows[:, :own].T)
    own_at = np.zeros((own, 2 * LANES), np.int32)
    own_at[:, :LANES] = spot_at[0, :own, None]
    own_at[:, LANES:] = spot_at[1, :own, None]
    return (
        pick.astype(jnp.bfloat16),
        own_rows.astype(jnp.bfloat16),
        own_at,
        spot_rows.astype(jnp.bfloat16),
        spot_at,
    )


def spot_of(row, col, rows, cols, half):
    own = rows * cols
    inner = (row >= 0) & (row < rows)
    mid = (col >= 0) & (col < cols)
    side = jnp.where(col < 0, col + 2, col - cols)
    far = jnp.where(row < 0, row + 2, row - rows)
    right = (col >= cols).astype(jnp.int32)
    down = (row >= rows).astype(jnp.int32)
    second = (col >= half).astype(jnp.int32)
    at_own = second * (rows * half) + row * half + col - second * half
    at_side = own + right * (2 * rows) + row * 2 + side
    base = own + 4 * rows
    at_far = base + down * (2 * cols) + far * cols + col
    at_corner = base + 4 * cols + (down * 2 + right) * 8 + far * 2 + side
    return jnp.where(
        inner, jnp.where(mid, at_own, at_side), jnp.where(mid, at_far, at_corner)
    )


def step_kernel(
    sizes,
    table_ref,
    pick_ref,
    own_rows_ref,
    own_at_ref,
    spot_rows_ref,
    spot_at_ref,
    in_ref,
    cot_ref,
    w_ref,
    out_ref,
    grad_ref,
    wg_ref,
    xp,
    gp,
    gown,
    hb,
    ahead,
    back,
    spread,
    spread_other,
    gate_other,
    slope,
    ob,
    gb,
    feat,
    product,
    blk,
    ysend,
    yrecv,
    acc,
    zsend,
    zrecv,
    fsend,
    frecv,
    cin_s,
    cin_r,
    hop_s,
    hop_r,
    halo_s,
    halo_r,
    oc_s,
    oc_r,
    pair_s,
    pair_r,
    y_s,
    y_r,
    z_s,
    z_r,
):
    n_seg, n_lat, n_z, scale = sizes
    half_cells, channels = in_ref.shape[1:]
    rows = table_ref.shape[0] - 16
    rows = rows // n_lat
    half = half_cells // rows
    cols = 2 * half
    own = rows * cols
    spots = 2 * own
    ring = 2 * n_lat
    steps = ring // 2
    share = BASIS * channels // (n_z * ring * 2)
    wide = channels // 2

    lon = lax.axis_index("lon")
    lat = lax.axis_index("lat")
    seg = lax.axis_index("segment")
    z = lon // 4
    member = (lon // 2) % 2
    core = lon % 2
    pos = z * 2 + core
    y = member * n_lat + lat

    def at(z_to, member_to, core_to, lat_to, seg_to=seg):
        return {"lon": z_to * 4 + member_to * 2 + core_to, "lat": lat_to, "segment": seg_to}

    def beside(shift, lat_to):
        place = lax.rem(pos + shift + 2 * n_z, 2 * n_z)
        return at(place // 2, member, place % 2, lat_to)

    has_up = lat > 0
    has_down = lat < n_lat - 1
    is_first = seg == 0
    is_last = seg == n_seg - 1
    matched = core == member

    base = 4 * rows
    corner = base + 4 * cols
    halo = [
        (0, 2 * rows, 1, 0),
        (2 * rows, 2 * rows, -1, 0),
        (base, 2 * cols, 0, 1),
        (base + 2 * cols, 2 * cols, 0, -1),
        (corner, 8, 1, 1),
        (corner + 8, 8, -1, 1),
        (corner + 16, 8, 1, -1),
        (corner + 24, 8, -1, -1),
    ]

    def sends_to(dlat):
        return has_down if dlat > 0 else has_up

    def gets_from(dlat):
        return has_up if dlat > 0 else has_down

    ring_next = lax.rem(y + 1, ring)
    ring_prev = lax.rem(y + ring - 1, ring)

    def on_ring(place):
        return at(z, place // n_lat, core, lax.rem(place, n_lat))

    partner = at(z, member, 1 - core, lat)

    barrier = pltpu.get_barrier_semaphore()

    def greet(device):
        pl.semaphore_signal(barrier, inc=1, device_id=device, device_id_type=MESH)

    for shift in range(1, n_z):
        greet(at(lax.rem(z + shift, n_z), member, core, lat))
    greet(on_ring(ring_next))
    greet(on_ring(ring_prev))
    greet(partner)
    for _, _, shift, dlat in halo:
        if dlat == 0:
            greet(beside(shift, lat))
        else:

            @pl.when(sends_to(dlat))
            def _():
                greet(beside(shift, lat + dlat))

    for other in range(2):

        @pl.when(jnp.logical_not(matched & (member == other)))
        def _():
            greet(at(z, other, member, lat))

        @pl.when(jnp.logical_not(matched & (core == other)))
        def _():
            greet(at(z, core, other, lat))

    @pl.when(jnp.logical_not(is_first))
    def _():
        greet(at(z, member, core, lat, seg - 1))

    @pl.when(jnp.logical_not(is_last))
    def _():
        greet(at(z, member, core, lat, seg + 1))

    met = (n_z - 1) + 3 + 2 + 4
    met = met + jnp.where(has_up, 3, 0) + jnp.where(has_down, 3, 0)
    met = met - jnp.where(matched, 2, 0)
    met = met + jnp.where(is_first, 0, 1) + jnp.where(is_last, 0, 1)
    pl.semaphore_wait(barrier, met)

    def remote(src, dst, send_sem, recv_sem, device):
        return pltpu.make_async_remote_copy(
            src_ref=src,
            dst_ref=dst,
            send_sem=send_sem,
            recv_sem=recv_sem,
            device_id=device,
            device_id_type=MESH,
        )

    def slot_of(buffer, part):
        return buffer.at[pl.ds(pl.multiple_of(part * half_cells, half_cells), half_cells), :]

    def regroup(source, buffer, which):
        for to in range(2):
            there = matched & (member == to)

            @pl.when(there)
            def _():
                pltpu.make_async_copy(
                    source.at[to], slot_of(buffer, core), cin_r.at[which, core]
                ).start()

            @pl.when(jnp.logical_not(there))
            def _():
                remote(
                    source.at[to],
                    slot_of(buffer, core),
                    cin_s.at[which, to],
                    cin_r.at[which, core],
                    at(z, to, member, lat),
                ).start()

    def regroup_arrived(source, buffer, which):
        for part in range(2):
            here = matched & (core == part)

            @pl.when(here)
            def _():
                pltpu.make_async_copy(
                    source.at[0], slot_of(buffer, part), cin_r.at[which, part]
                ).wait()

            @pl.when(jnp.logical_not(here))
            def _():
                remote(
                    source.at[0],
                    slot_of(buffer, part),
                    cin_s.at[which, 0],
                    cin_r.at[which, part],
                    partner,
                ).wait_recv()

    def regroup_sent(source, buffer, which):
        for to in range(2):

            @pl.when(jnp.logical_not(matched & (member == to)))
            def _():
                remote(
                    source.at[to],
                    slot_of(buffer, core),
                    cin_s.at[which, to],
                    cin_r.at[which, core],
                    partner,
                ).wait_send()

    @pl.when(is_first)
    def _():
        regroup(in_ref, xp, 0)

    @pl.when(is_last)
    def _():
        regroup(cot_ref, gown, 1)

    for buffer in (xp, gp):

        @pl.when(jnp.logical_not(has_up))
        def _():
            buffer[pl.ds(own + base, 2 * cols), :] = jnp.zeros((2 * cols, channels), BF16)
            buffer[pl.ds(own + corner, 16), :] = jnp.zeros((16, channels), BF16)

        @pl.when(jnp.logical_not(has_down))
        def _():
            buffer[pl.ds(own + base + 2 * cols, 2 * cols), :] = jnp.zeros((2 * cols, channels), BF16)
            buffer[pl.ds(own + corner + 16, 16), :] = jnp.zeros((16, channels), BF16)

    near_rows = rows + 8
    near = table_ref[pl.ds(pl.multiple_of(lat * rows, rows), near_rows), :]
    told = jnp.dot(own_rows_ref[...], near.astype(BF16), preferred_element_type=F32)
    tap_row = told[:, :LANES].astype(jnp.int32) + own_at_ref[:, :LANES]
    tap_col = told[:, LANES : 2 * LANES].astype(jnp.int32) + own_at_ref[:, LANES:]
    in_grid = (tap_row + lat * rows >= 0) & (tap_row + lat * rows < n_lat * rows)
    source = jnp.where(in_grid, spot_of(tap_row, tap_col, rows, cols, half), -1)
    lane = lax.broadcasted_iota(jnp.int32, (own, spots), 1)
    totals = [jnp.zeros((own, spots), F32) for _ in range(BASIS)]
    for tap in range(TAPS):
        hit = lane == source[:, tap : tap + 1]
        for b in range(BASIS):
            at_lane = 2 * LANES + b * TAPS + tap
            totals[b] = totals[b] + jnp.where(hit, told[:, at_lane : at_lane + 1], 0.0)
    for b in range(BASIS):
        ahead[pl.ds(b * own, own), :] = totals[b].astype(BF16)

    told_back = jnp.dot(
        jnp.transpose(near).astype(BF16), spot_rows_ref[...], preferred_element_type=F32
    )
    spot_row = jnp.broadcast_to(spot_at_ref[0:1, :], (16, spots))
    spot_col = jnp.broadcast_to(spot_at_ref[1:2, :], (16, spots))
    to_row = told_back[:16].astype(jnp.int32) + spot_row
    to_col = told_back[LANES : LANES + 16].astype(jnp.int32) + spot_col
    lands = (to_row >= 0) & (to_row < rows) & (to_col >= 0) & (to_col < cols)
    second = (to_col >= half).astype(jnp.int32)
    target = jnp.where(
        lands, second * (rows * half) + to_row * half + to_col - second * half, -1
    )
    level = lax.broadcasted_iota(jnp.int32, (own, spots), 0)
    totals = [jnp.zeros((own, spots), F32) for _ in range(BASIS)]
    for tap in range(TAPS):
        hit = level == target[tap : tap + 1, :]
        for b in range(BASIS):
            at_row = 2 * LANES + b * TAPS + tap
            totals[b] = totals[b] + jnp.where(hit, told_back[at_row : at_row + 1, :], 0.0)
    for b in range(BASIS):
        back[:, pl.ds(b * spots, spots)] = totals[b].astype(BF16)

    def halo_copy(buffer, phase, number):
        start, size, shift, dlat = halo[number]
        return remote(
            hb.at[phase, pl.ds(start, size), :],
            buffer.at[pl.ds(own + start, size), :],
            halo_s.at[phase, number],
            halo_r.at[phase, number],
            beside(shift, lat + dlat),
        )

    def halo_start(block, buffer, phase):
        hb[phase] = jnp.dot(pick_ref[...], block, preferred_element_type=F32).astype(BF16)
        for number in (4, 5, 6, 7, 2, 3, 0, 1):
            dlat = halo[number][3]
            if dlat == 0:
                halo_copy(buffer, phase, number).start()
            else:

                @pl.when(sends_to(dlat))
                def _():
                    halo_copy(buffer, phase, number).start()

    def halo_arrived(buffer, phase):
        for number in range(8):
            dlat = halo[number][3]
            if dlat == 0:
                halo_copy(buffer, phase, number).wait_recv()
            else:

                @pl.when(gets_from(dlat))
                def _():
                    halo_copy(buffer, phase, number).wait_recv()

    def halo_sent(buffer, phase):
        for number in range(8):
            dlat = halo[number][3]
            if dlat == 0:
                halo_copy(buffer, phase, number).wait_send()
            else:

                @pl.when(sends_to(dlat))
                def _():
                    halo_copy(buffer, phase, number).wait_send()

    def restore_copy(block, output, which, part, arrives_from):
        return remote(
            block.at[pl.ds(part * half_cells, half_cells), :],
            output.at[arrives_from],
            oc_s.at[which, part],
            oc_r.at[which, arrives_from],
            at(z, core, part, lat),
        )

    def restore_start(block, output, which):
        for part in range(2):
            there = matched & (core == part)

            @pl.when(there)
            def _():
                pltpu.make_async_copy(
                    block.at[pl.ds(part * half_cells, half_cells), :],
                    output.at[member],
                    oc_r.at[which, member],
                ).start()

            @pl.when(jnp.logical_not(there))
            def _():
                restore_copy(block, output, which, part, member).start()

    def restore_finish(block, output, which):
        for part in range(2):

            @pl.when(jnp.logical_not(matched & (core == part)))
            def _():
                restore_copy(block, output, which, part, member).wait_send()

        for origin in range(2):
            here = matched & (member == origin)

            @pl.when(here)
            def _():
                pltpu.make_async_copy(
                    block.at[pl.ds(0, half_cells), :],
                    output.at[origin],
                    oc_r.at[which, origin],
                ).wait()

            @pl.when(jnp.logical_not(here))
            def _():
                restore_copy(block, output, which, 0, origin).wait_recv()

    def hop_ahead():
        return remote(
            ob, xp.at[pl.ds(0, own), :], hop_s.at[0], hop_r.at[0], at(z, member, core, lat, seg + 1)
        )

    def hop_back():
        return remote(
            gb, gown, hop_s.at[1], hop_r.at[1], at(z, member, core, lat, seg - 1)
        )

    @pl.when(is_first)
    def _():
        regroup_arrived(in_ref, xp, 0)

    @pl.when(jnp.logical_not(is_first))
    def _():
        hop_ahead().wait_recv()

    halo_start(xp[pl.ds(0, own), :], xp, 0)
    halo_arrived(xp, 0)
    widened = xp[...]
    for b in range(BASIS):
        spread[pl.ds(b * own, own), :] = jnp.dot(
            ahead[pl.ds(b * own, own), :], widened, preferred_element_type=F32
        ).astype(BF16)
    mixed = jnp.dot(spread[pl.ds(0, own), :], w_ref[0], preferred_element_type=F32)
    for b in range(1, BASIS):
        mixed = mixed + jnp.dot(
            spread[pl.ds(b * own, own), :], w_ref[b], preferred_element_type=F32
        )
    sigma = 1.0 / (1.0 + jnp.exp(-mixed))
    ob[...] = (xp[pl.ds(0, own), :].astype(F32) + mixed * sigma).astype(BF16)

    @pl.when(jnp.logical_not(is_last))
    def _():
        hop_ahead().start()

    slope[...] = sigma * (1.0 + mixed * (1.0 - sigma))
    restore_start(ob, out_ref, 0)
    pair_spread = remote(spread, spread_other, pair_s.at[0], pair_r.at[0], partner)
    pair_spread.start()

    @pl.when(is_last)
    def _():
        regroup_arrived(cot_ref, gown, 1)

    @pl.when(jnp.logical_not(is_last))
    def _():
        hop_back().wait_recv()

    gate = (gown[...].astype(F32) * slope[...]).astype(BF16)
    gp[pl.ds(0, own), :] = gate
    halo_start(gate, gp, 1)
    pair_gate = remote(gp.at[pl.ds(0, own), :], gate_other, pair_s.at[1], pair_r.at[1], partner)
    pair_gate.start()
    pair_spread.wait_recv()
    pair_gate.wait_recv()

    columns = pl.ds(pl.multiple_of(core * wide, wide), wide)
    gate_both = jnp.concatenate(
        [gp[pl.ds(0, own), columns], gate_other[:, columns]], axis=0
    )
    for b in range(BASIS):
        both = jnp.concatenate(
            [spread[pl.ds(b * own, own), :], spread_other[pl.ds(b * own, own), :]], axis=0
        )
        term = scale * lax.dot_general(
            both, gate_both, (((0,), (0,)), ((), ())), preferred_element_type=F32
        )
        for part in range(wide // LANES):
            product[part, pl.ds(b * channels, channels), :] = term[
                :, part * LANES : (part + 1) * LANES
            ]

    halo_arrived(gp, 1)
    for b in range(BASIS):
        feat[pl.ds(b * spots, spots), :] = lax.dot_general(
            gp[...], w_ref[b], (((1,), (1,)), ((), ())), preferred_element_type=F32
        ).astype(BF16)
    pulled = jnp.dot(back[...], feat[...], preferred_element_type=F32)
    gb[...] = (gown[...].astype(F32) + pulled).astype(BF16)

    @pl.when(jnp.logical_not(is_first))
    def _():
        hop_back().start()

    restore_start(gb, grad_ref, 1)

    group = share * n_z
    for place in range(ring):
        for e in range(2):
            for i in range(share):
                first = ((place // n_lat) * 2 + e) * n_lat * share + (place % n_lat) * share + i
                for part in range(wide // LANES):
                    blk[place, pl.ds(e * group + i * n_z, n_z), pl.ds(part * LANES, LANES)] = product[
                        part, pl.ds(first, n_z, stride=ring * 2 * share), :
                    ].astype(BF16)

    def ring_copy(way, step):
        lo, size = (0, 2 * group) if step else (way * group, group)
        return remote(
            ysend.at[way, step, pl.ds(lo, size), :],
            yrecv.at[way, step, pl.ds(lo, size), :],
            y_s.at[way, step],
            y_r.at[way, step],
            on_ring(ring_next if way == 0 else ring_prev),
        )

    for step in range(steps):
        for way in range(2):
            distance = steps - step
            place = lax.rem(y + (distance if way == 0 else ring - distance), ring)
            if step == 0:
                lo = way * group
                ysend[way, step, pl.ds(lo, group), :] = blk[place, pl.ds(lo, group), :]
            else:
                ring_copy(way, step - 1).wait_recv()
                if step == 1:
                    lo, rest = way * group, (1 - way) * group
                    ysend[way, step, pl.ds(lo, group), :] = (
                        blk[place, pl.ds(lo, group), :].astype(F32)
                        + yrecv[way, 0, pl.ds(lo, group), :].astype(F32)
                    ).astype(BF16)
                    ysend[way, step, pl.ds(rest, group), :] = blk[place, pl.ds(rest, group), :]
                else:
                    ysend[way, step] = (
                        blk[place].astype(F32) + yrecv[way, step - 1].astype(F32)
                    ).astype(BF16)
            ring_copy(way, step).start()
    summed = blk[y].astype(F32)
    for way in range(2):
        ring_copy(way, steps - 1).wait_recv()
        summed = summed + yrecv[way, steps - 1].astype(F32)
    for part in range(wide // LANES):
        acc[part] = summed[:, part * LANES : (part + 1) * LANES]

    def z_copy(shift):
        to = lax.rem(z + shift, n_z)
        return remote(
            zsend.at[to], zrecv.at[z], z_s.at[shift], z_r.at[shift], at(to, member, core, lat)
        )

    for to in range(n_z):
        for part in range(wide // LANES):
            zsend[to, pl.ds(0, 2 * share), pl.ds(part * LANES, LANES)] = acc[
                part, pl.ds(to, 2 * share, stride=n_z), :
            ].astype(BF16)
    for shift in range(1, n_z):
        z_copy(shift).start()
    total = zsend[z][: 2 * share].astype(F32)
    for shift in range(1, n_z):
        from_z = lax.rem(z + n_z - shift, n_z)
        remote(
            zsend.at[0], zrecv.at[from_z], z_s.at[shift], z_r.at[shift], partner
        ).wait_recv()
        total = total + zrecv[from_z][: 2 * share].astype(F32)
    mine = jnp.where(core == 0, total[:share], total[share:])
    fsend[pl.ds(0, share), :] = jnp.where(core == 0, total[share:], total[:share])
    last = remote(fsend, frecv, pair_s.at[2], pair_r.at[2], partner)
    last.start()
    last.wait_recv()
    theirs = frecv[pl.ds(0, share), :]
    wg_ref[:, :wide] = jnp.where(core == 0, mine, theirs)
    wg_ref[:, wide:] = jnp.where(core == 0, theirs, mine)

    restore_finish(ob, out_ref, 0)
    restore_finish(gb, grad_ref, 1)

    @pl.when(is_first)
    def _():
        regroup_sent(in_ref, xp, 0)

    @pl.when(is_last)
    def _():
        regroup_sent(cot_ref, gown, 1)

    @pl.when(jnp.logical_not(is_last))
    def _():
        hop_ahead().wait_send()

    @pl.when(jnp.logical_not(is_first))
    def _():
        hop_back().wait_send()

    halo_sent(xp, 0)
    halo_sent(gp, 1)
    pair_spread.wait_send()
    pair_gate.wait_send()
    last.wait_send()
    for step in range(steps):
        for way in range(2):
            ring_copy(way, step).wait_send()
    for shift in range(1, n_z):
        z_copy(shift).wait_send()


def per_device(inputs, cotangent, weights, basis_values, lat_step, lon_step):
    members, rows, half, channels = inputs.shape
    n_lon, n_lat, n_seg = (lax.axis_size(name) for name in ("lon", "lat", "segment"))
    n_z = n_lon // 4
    cols = 2 * half
    own = rows * cols
    spots = 2 * own
    ring = 2 * n_lat
    share = BASIS * channels // (n_lon * n_lat)
    wide = channels // 2
    scale = 1.0 / math.sqrt(members * rows * n_lat * half * n_lon)

    def padded(table):
        table = table.astype(F32)
        return jnp.pad(table, ((REACH, 16 - REACH), (0, LANES - table.shape[1])))

    by_basis = jnp.transpose(basis_values, (0, 2, 1)).reshape(rows * n_lat, BASIS * TAPS)
    table = jnp.concatenate([padded(lat_step), padded(lon_step), padded(by_basis)], axis=1)
    constants = [jnp.asarray(t) for t in static_tables(rows, cols, half)]
    vmem = pl.BlockSpec(memory_space=pltpu.VMEM)
    dma = pltpu.SemaphoreType.DMA
    section_out, section_grad, weight_grad = pl.pallas_call(
        functools.partial(step_kernel, (n_seg, n_lat, n_z, scale)),
        out_shape=(
            jax.ShapeDtypeStruct((2, rows * half, channels), BF16),
            jax.ShapeDtypeStruct((2, rows * half, channels), BF16),
            jax.ShapeDtypeStruct((share, channels), F32),
        ),
        in_specs=[vmem] * 9,
        out_specs=(vmem, vmem, vmem),
        scratch_shapes=[
            pltpu.VMEM((spots, channels), BF16),
            pltpu.VMEM((spots, channels), BF16),
            pltpu.VMEM((own, channels), BF16),
            pltpu.VMEM((2, own, channels), BF16),
            pltpu.VMEM((BASIS * own, spots), BF16),
            pltpu.VMEM((own, BASIS * spots), BF16),
            pltpu.VMEM((BASIS * own, channels), BF16),
            pltpu.VMEM((BASIS * own, channels), BF16),
            pltpu.VMEM((own, channels), BF16),
            pltpu.VMEM((own, channels), F32),
            pltpu.VMEM((own, channels), BF16),
            pltpu.VMEM((own, channels), BF16),
            pltpu.VMEM((BASIS * spots, channels), BF16),
            pltpu.VMEM((wide // LANES, BASIS * channels, LANES), F32),
            pltpu.VMEM((ring, 2 * share * n_z, wide), BF16),
            pltpu.VMEM((2, n_lat, 2 * share * n_z, wide), BF16),
            pltpu.VMEM((2, n_lat, 2 * share * n_z, wide), BF16),
            pltpu.VMEM((wide // LANES, 2 * share * n_z, LANES), F32),
            pltpu.VMEM((n_z, -(-2 * share // 16) * 16, wide), BF16),
            pltpu.VMEM((n_z, -(-2 * share // 16) * 16, wide), BF16),
            pltpu.VMEM((-(-share // 8) * 8, wide), F32),
            pltpu.VMEM((-(-share // 8) * 8, wide), F32),
            dma((2, 2)),
            dma((2, 2)),
            dma((2,)),
            dma((2,)),
            dma((2, 8)),
            dma((2, 8)),
            dma((2, 2)),
            dma((2, 2)),
            dma((3,)),
            dma((3,)),
            dma((2, n_lat)),
            dma((2, n_lat)),
            dma((n_z,)),
            dma((n_z,)),
        ],
        compiler_params=pltpu.CompilerParams(
            collective_id=0, has_side_effects=True, vmem_limit_bytes=48 * 1024 * 1024
        ),
        name="section_step",
    )(
        table,
        *constants,
        inputs.reshape(members, rows * half, channels),
        cotangent.reshape(members, rows * half, channels),
        weights[0],
    )
    block = (1,) + inputs.shape
    return (
        section_out.reshape(block),
        section_grad.reshape(block),
        weight_grad.reshape(1, -1),
    )


def solution(mesh):
    return jax.shard_map(
        per_device,
        mesh=mesh,
        in_specs=(
            P(None, "lat", "lon", None),
            P(None, "lat", "lon", None),
            P("segment", None, None, None),
            P(),
            P(),
            P(),
        ),
        out_specs=(
            P("segment", None, "lat", "lon", None),
            P("segment", None, "lat", "lon", None),
            P("segment", ("lon", "lat")),
        ),
        check_vma=False,
    )
```

time: 643 us -> 134 us (0.21)
  waiting for transfers between devices: 389 us -> 0 us
  starting transfers between devices: 181 us -> 0 us
  Pallas kernels: 0 us -> 121 us
  matrix products: 19.4 us -> 0 us
  between operations: 15.1 us -> 0.66 us
  other arithmetic: 14.1 us -> 1.41 us
  local copies, waits for them, and re-layouts: 21.7 us -> 10.1 us
    unnamed x2 -> x0, waiting for transfers between devices: 329 us -> none
    ppermute x38 -> x0, starting transfers between devices: 181 us -> none  [the longest x16 124 us: with_halo(): after = lax.ppermute(first, axis, down)]
    pallas_call x0 -> x1, Pallas kernels: none -> 121 us  [per_device(): pl.pallas_call(functools.partial(step_kernel, (n_seg, n_lat, n_z, scale))...]
    ppermute x38 -> x0, waiting for transfers between devices: 60 us -> none  [the longest x16 38.9 us: with_halo(): before = lax.ppermute(last, axis, up)]
    dot_general x19 -> x0, matrix products: 19.4 us -> none  [the longest x4 4.28 us: per_device(): jnp.einsum('bts,msc->bmtc', forward_map, layer_padded, precision=lax.Prec...]
  transfers between devices with their start and end apart: 39 -> 0, of which waited for: 26 -> 0; matrix products, arithmetic and copies ran while one was open for 3% -> 0% of each run, Pallas kernels for 0% -> 0%
where the time goes in v1:
time: 134 us; the launch traced here: 133 us
  Pallas kernels  121 us (90%)
  local copies, waits for them, and re-layouts  10.1 us (8%)
  other arithmetic  1.41 us (1%)
    pallas_call x1, Pallas kernels, per_device(): pl.pallas_call(functools.partial(step_kernel, (n_seg, n_lat, n_z, scale))...  121 us
    unnamed x13, local copies, waits for them, and re-layouts  5.86 us

profile of v1, /device:TPU:1, one launch (start us, length us, event | category | flops | bytes accessed | tf_op | source)
XLA Modules:
  0.0 132.9 jit_solution(1855497505139346006)
XLA Ops:
  0.6 0.7 convert_element_type.11
  1.3 0.7 convert_element_type.12
  2.0 0.1 copy.22
  2.1 0.1 copy.21
  2.2 0.7 copy.23
  3.0 0.1 copy.24
  3.1 0.9 reshape.25.in_ref
  4.0 0.9 reshape.26.cot_ref
  5.0 0.0 copy-start
  5.0 1.4 %copy-done = bf16[1,3,512,512]{3,2,1,0:T(8,128)(2,1)S(1)} copy-done((bf16[1,3,512,512]{3,2,1,0:T(8,128)(2,1)S(1)}, bf16[1,3,512,512]{3,2,1,0:T(8,128)(2,1)}, u32[]{:S(2)}) %copy-start) | copy-done | bytes 1572888
  6.4 0.0 copy-start.1
  6.4 0.9 copy-done.1
  7.3 0.0 copy-start.2
  7.3 0.8 copy-done.2
  8.0 0.0 copy-start.3
  8.0 0.8 copy-done.3
  8.8 0.0 copy-start.4
  8.8 0.7 copy-done.4
  9.5 0.0 copy-start.5
  9.5 0.7 copy-done.5
  10.2 120.7 %section_step.1 = (bf16[2,64,512]{2,1,0:T(8,128)(2,1)S(1)}, bf16[2,64,512]{2,1,0:T(8,128)(2,1)S(1)}, f32[6,512]{1,0:T(8,128)S(1)}) custom-call(f32[80,384]{1,0:T(8,128)S(1)} %select_maximum_fusion.table_ref, bf16[128,128]{1,0:T(8,128)(2,1)S(1)} %copy-done.3, bf16[128,24]{1,0:T(8,128)(2,1)S(1)} %copy-done.2, s32[128,256]{1,0:T(8,128)S(1)} %copy-done.1, ...), custom_call_target="tpu_custom_call" | custom-call | tf_op jit(solution)/shard_map/section_step/pallas_call | solution.py:677
  130.9 0.7 reshape.27
  131.6 0.6 copy.25
  132.2 0.7 reshape.28
  (2 shorter events, 0.0 us)
Async XLA Ops:
  5.0 1.4 %copy-start = (bf16[1,3,512,512]{3,2,1,0:T(8,128)(2,1)S(1)}, bf16[1,3,512,512]{3,2,1,0:T(8,128)(2,1)}, u32[]{:S(2)}) copy-start(bf16[1,3,512,512]{3,2,1,0:T(8,128)(2,1)} %param.13) | copy-start | bytes 4718596
  6.4 0.9 copy-start.1
  7.3 0.8 copy-start.2
  8.0 0.8 copy-start.3
  8.8 0.7 copy-start.4
  9.5 0.7 copy-start.5

commit v2 on v1

--- a/solution.py
+++ b/solution.py
@@ -3,7 +3,6 @@
 
 import jax
 import jax.numpy as jnp
-import numpy as np
 from jax import lax
 from jax.experimental import pallas as pl
 from jax.experimental.pallas import tpu as pltpu
@@ -18,52 +17,44 @@
 BF16 = jnp.bfloat16
 
 
-def cell_index(row, col, rows, half):
-    return (col // half) * (rows * half) + row * half + col % half
-
-
-def halo_cells(rows, cols):
-    cells = []
-    for col in (-2, cols):
-        cells += [(i, col + j) for i in range(rows) for j in range(2)]
-    for row in (-2, rows):
-        cells += [(row + i, j) for i in range(2) for j in range(cols)]
-    for row in (-2, rows):
-        for col in (-2, cols):
-            cells += [(row + i, col + j) for i in range(2) for j in range(2)] + [None] * 4
-    return cells
-
-
-def static_tables(rows, cols, half):
-    own = rows * cols
-    cells = [None] * own
-    for i in range(rows):
-        for j in range(cols):
-            cells[cell_index(i, j, rows, half)] = (i, j)
-    halo = halo_cells(rows, cols)
-    pick = np.zeros((len(halo), own), np.float32)
-    for slot, cell in enumerate(halo):
-        if cell is not None:
-            pick[slot, cell_index(cell[0] % rows, cell[1] % cols, rows, half)] = 1
-    near = rows + 8
-    spots = cells + halo
-    spot_rows = np.zeros((near, len(spots)), np.float32)
-    spot_at = np.full((16, len(spots)), -100, np.int32)
-    for s, cell in enumerate(spots):
-        if cell is not None:
-            spot_rows[cell[0] + REACH, s] = 1
-            spot_at[0, s], spot_at[1, s] = cell
-    own_rows = np.ascontiguousarray(spot_rows[:, :own].T)
-    own_at = np.zeros((own, 2 * LANES), np.int32)
-    own_at[:, :LANES] = spot_at[0, :own, None]
-    own_at[:, LANES:] = spot_at[1, :own, None]
-    return (
-        pick.astype(jnp.bfloat16),
-        own_rows.astype(jnp.bfloat16),
-        own_at,
-        spot_rows.astype(jnp.bfloat16),
-        spot_at,
-    )
+def log2(number):
+    power = number.bit_length() - 1
+    assert 1 << power == number
+    return power
+
+
+def over(x, number):
+    return lax.shift_right_arithmetic(x, jnp.full_like(x, log2(number)))
+
+
+def rest(x, number):
+    return x & (number - 1)
+
+
+def halo_cell(slot, rows, cols):
+    base = 4 * rows
+    at = slot
+    side_row = over(rest(at, 2 * rows), 2)
+    side_col = rest(at, 2) + jnp.where(at < 2 * rows, -2, cols)
+    at = slot - base
+    far_row = over(rest(at, 2 * cols), cols) + jnp.where(at < 2 * cols, -2, rows)
+    far_col = rest(at, cols)
+    at = slot - base - 4 * cols
+    inside = rest(at, 8)
+    corner_row = over(inside, 2) + jnp.where(at < 16, -2, rows)
+    corner_col = rest(inside, 2) + jnp.where(rest(over(at, 8), 2) == 0, -2, cols)
+    in_side = slot < base
+    in_far = slot < base + 4 * cols
+    row = jnp.where(in_side, side_row, jnp.where(in_far, far_row, corner_row))
+    col = jnp.where(in_side, side_col, jnp.where(in_far, far_col, corner_col))
+    used = in_far | (inside < 4)
+    return row, col, used
+
+
+def own_cell(spot, rows, half):
+    second = over(spot, rows * half)
+    at = rest(spot, rows * half)
+    return over(at, half), rest(at, half) + second * half
 
 
 def spot_of(row, col, rows, cols, half):
@@ -87,18 +78,21 @@
 
 def step_kernel(
     sizes,
-    table_ref,
-    pick_ref,
-    own_rows_ref,
-    own_at_ref,
-    spot_rows_ref,
-    spot_at_ref,
+    lat_hbm,
+    lon_hbm,
+    basis_hbm,
     in_ref,
     cot_ref,
-    w_ref,
+    w_hbm,
     out_ref,
     grad_ref,
     wg_ref,
+    lat_ref,
+    lon_ref,
+    basis_ref,
+    w_ref,
+    raw,
+    pick,
     xp,
     gp,
     gown,
@@ -135,12 +129,11 @@
     y_r,
     z_s,
     z_r,
+    w_sem,
 ):
     n_seg, n_lat, n_z, scale = sizes
-    half_cells, channels = in_ref.shape[1:]
-    rows = table_ref.shape[0] - 16
-    rows = rows // n_lat
-    half = half_cells // rows
+    rows, half, channels = in_ref.shape[1:]
+    half_cells = rows * half
     cols = 2 * half
     own = rows * cols
     spots = 2 * own
@@ -198,6 +191,17 @@
 
     partner = at(z, member, 1 - core, lat)
 
+    fetch = pltpu.make_async_copy(w_hbm, w_ref, w_sem.at[0])
+    tables = [
+        pltpu.make_async_copy(table_hbm, table_ref, w_sem.at[1 + number])
+        for number, (table_hbm, table_ref) in enumerate(
+            ((lat_hbm, lat_ref), (lon_hbm, lon_ref), (basis_hbm, basis_ref))
+        )
+    ]
+    for table in tables:
+        table.start()
+    fetch.start()
+
     barrier = pltpu.get_barrier_semaphore()
 
     def greet(device):
@@ -252,7 +256,7 @@
         )
 
     def slot_of(buffer, part):
-        return buffer.at[pl.ds(pl.multiple_of(part * half_cells, half_cells), half_cells), :]
+        return buffer.at[part]
 
     def regroup(source, buffer, which):
         for to in range(2):
@@ -309,11 +313,11 @@
 
     @pl.when(is_first)
     def _():
-        regroup(in_ref, xp, 0)
+        regroup(in_ref, raw.at[0], 0)
 
     @pl.when(is_last)
     def _():
-        regroup(cot_ref, gown, 1)
+        regroup(cot_ref, raw.at[1], 1)
 
     for buffer in (xp, gp):
 
@@ -327,30 +331,29 @@
             buffer[pl.ds(own + base + 2 * cols, 2 * cols), :] = jnp.zeros((2 * cols, channels), BF16)
             buffer[pl.ds(own + corner + 16, 16), :] = jnp.zeros((16, channels), BF16)
 
-    near_rows = rows + 8
-    near = table_ref[pl.ds(pl.multiple_of(lat * rows, rows), near_rows), :]
-    told = jnp.dot(own_rows_ref[...], near.astype(BF16), preferred_element_type=F32)
-    tap_row = told[:, :LANES].astype(jnp.int32) + own_at_ref[:, :LANES]
-    tap_col = told[:, LANES : 2 * LANES].astype(jnp.int32) + own_at_ref[:, LANES:]
-    in_grid = (tap_row + lat * rows >= 0) & (tap_row + lat * rows < n_lat * rows)
-    source = jnp.where(in_grid, spot_of(tap_row, tap_col, rows, cols, half), -1)
-    lane = lax.broadcasted_iota(jnp.int32, (own, spots), 1)
-    totals = [jnp.zeros((own, spots), F32) for _ in range(BASIS)]
-    for tap in range(TAPS):
-        hit = lane == source[:, tap : tap + 1]
-        for b in range(BASIS):
-            at_lane = 2 * LANES + b * TAPS + tap
-            totals[b] = totals[b] + jnp.where(hit, told[:, at_lane : at_lane + 1], 0.0)
-    for b in range(BASIS):
-        ahead[pl.ds(b * own, own), :] = totals[b].astype(BF16)
-
-    told_back = jnp.dot(
-        jnp.transpose(near).astype(BF16), spot_rows_ref[...], preferred_element_type=F32
-    )
-    spot_row = jnp.broadcast_to(spot_at_ref[0:1, :], (16, spots))
-    spot_col = jnp.broadcast_to(spot_at_ref[1:2, :], (16, spots))
-    to_row = told_back[:16].astype(jnp.int32) + spot_row
-    to_col = told_back[LANES : LANES + 16].astype(jnp.int32) + spot_col
+    spot = lax.broadcasted_iota(jnp.int32, (16, spots), 1)
+    inner_row, inner_col = own_cell(spot, rows, half)
+    outer_row, outer_col, used = halo_cell(spot - own, rows, cols)
+    spot_row = jnp.where(spot < own, inner_row, outer_row)
+    spot_col = jnp.where(spot < own, inner_col, outer_col)
+    used = (spot < own) | used
+    grid_row = jnp.where(used, spot_row + lat * rows, -1)[:1]
+    total_rows = n_lat * rows
+    chosen = (
+        lax.broadcasted_iota(jnp.int32, (total_rows, spots), 0)
+        == jnp.broadcast_to(grid_row, (total_rows, spots))
+    ).astype(F32).astype(BF16)
+
+    for table in tables:
+        table.wait()
+
+    def of_spot(taps):
+        return jnp.dot(taps.astype(F32).astype(BF16), chosen, preferred_element_type=F32)
+
+    to_row = of_spot(lat_ref[...]).astype(jnp.int32) + spot_row[:TAPS]
+    to_col = of_spot(lon_ref[...]).astype(jnp.int32) + spot_col[:TAPS]
+    worth = [of_spot(basis_ref[:, b, :]) for b in range(BASIS)]
+
     lands = (to_row >= 0) & (to_row < rows) & (to_col >= 0) & (to_col < cols)
     second = (to_col >= half).astype(jnp.int32)
     target = jnp.where(
@@ -361,10 +364,30 @@
     for tap in range(TAPS):
         hit = level == target[tap : tap + 1, :]
         for b in range(BASIS):
-            at_row = 2 * LANES + b * TAPS + tap
-            totals[b] = totals[b] + jnp.where(hit, told_back[at_row : at_row + 1, :], 0.0)
+            totals[b] = totals[b] + jnp.where(hit, worth[b][tap : tap + 1, :], 0.0)
     for b in range(BASIS):
         back[:, pl.ds(b * spots, spots)] = totals[b].astype(BF16)
+
+    tap_row, tap_col = to_row[:, :own], to_col[:, :own]
+    in_grid = (tap_row + lat * rows >= 0) & (tap_row + lat * rows < total_rows)
+    source = jnp.where(in_grid, spot_of(tap_row, tap_col, rows, cols, half), -1)
+    level = lax.broadcasted_iota(jnp.int32, (spots, own), 0)
+    totals = [jnp.zeros((spots, own), F32) for _ in range(BASIS)]
+    for tap in range(TAPS):
+        hit = level == source[tap : tap + 1, :]
+        for b in range(BASIS):
+            totals[b] = totals[b] + jnp.where(hit, worth[b][tap : tap + 1, :own], 0.0)
+    for b in range(BASIS):
+        ahead[pl.ds(b * own, own), :] = jnp.transpose(totals[b]).astype(BF16)
+
+    slot = lax.broadcasted_iota(jnp.int32, (own, own), 0)
+    pick_row, pick_col, used = halo_cell(slot, rows, cols)
+    pick_row, pick_col = rest(pick_row, rows), rest(pick_col, cols)
+    wanted = over(pick_col, half) * (rows * half) + pick_row * half + rest(pick_col, half)
+    wanted = jnp.where(used, wanted, -1)
+    pick[...] = (
+        (lax.broadcasted_iota(jnp.int32, (own, own), 1) == wanted).astype(F32).astype(BF16)
+    )
 
     def halo_copy(buffer, phase, number):
         start, size, shift, dlat = halo[number]
@@ -377,7 +400,7 @@
         )
 
     def halo_start(block, buffer, phase):
-        hb[phase] = jnp.dot(pick_ref[...], block, preferred_element_type=F32).astype(BF16)
+        hb[phase] = jnp.dot(pick[...], block, preferred_element_type=F32).astype(BF16)
         for number in (4, 5, 6, 7, 2, 3, 0, 1):
             dlat = halo[number][3]
             if dlat == 0:
@@ -469,7 +492,8 @@
 
     @pl.when(is_first)
     def _():
-        regroup_arrived(in_ref, xp, 0)
+        regroup_arrived(in_ref, raw.at[0], 0)
+        xp[pl.ds(0, own), :] = raw[0].reshape(own, channels)
 
     @pl.when(jnp.logical_not(is_first))
     def _():
@@ -482,6 +506,7 @@
         spread[pl.ds(b * own, own), :] = jnp.dot(
             ahead[pl.ds(b * own, own), :], widened, preferred_element_type=F32
         ).astype(BF16)
+    fetch.wait()
     mixed = jnp.dot(spread[pl.ds(0, own), :], w_ref[0], preferred_element_type=F32)
     for b in range(1, BASIS):
         mixed = mixed + jnp.dot(
@@ -501,7 +526,8 @@
 
     @pl.when(is_last)
     def _():
-        regroup_arrived(cot_ref, gown, 1)
+        regroup_arrived(cot_ref, raw.at[1], 1)
+        gown[...] = raw[1].reshape(own, channels)
 
     @pl.when(jnp.logical_not(is_last))
     def _():
@@ -531,6 +557,44 @@
                 :, part * LANES : (part + 1) * LANES
             ]
 
+    group = share * n_z
+
+    def ring_copy(way, step, e):
+        return remote(
+            ysend.at[way, step, pl.ds(e * group, group), :],
+            yrecv.at[way, step, pl.ds(e * group, group), :],
+            y_s.at[way, step, e],
+            y_r.at[way, step, e],
+            on_ring(ring_next if way == 0 else ring_prev),
+        )
+
+    def ring_step(step, way, e):
+        distance = steps - step
+        place = lax.rem(y + (distance if way == 0 else ring - distance), ring)
+        part = pl.ds(e * group, group)
+        term = blk[place, part, :]
+        if step > 1 or (step == 1 and e == way):
+            ring_copy(way, step - 1, e).wait_recv()
+            term = (term.astype(F32) + yrecv[way, step - 1, part, :].astype(F32)).astype(BF16)
+        ysend[way, step, part, :] = term
+        ring_copy(way, step, e).start()
+
+    def ring_begin():
+        for place in range(ring):
+            for e in range(2):
+                for i in range(share):
+                    first = ((place // n_lat) * 2 + e) * n_lat * share + (place % n_lat) * share + i
+                    for part in range(wide // LANES):
+                        blk[
+                            place, pl.ds(e * group + i * n_z, n_z), pl.ds(part * LANES, LANES)
+                        ] = product[part, pl.ds(first, n_z, stride=ring * 2 * share), :].astype(BF16)
+        for way in range(2):
+            ring_step(0, way, way)
+        for way in range(2):
+            ring_step(1, way, 1 - way)
+
+    pl.when(is_first)(ring_begin)
+
     halo_arrived(gp, 1)
     for b in range(BASIS):
         feat[pl.ds(b * spots, spots), :] = lax.dot_general(
@@ -545,50 +609,17 @@
 
     restore_start(gb, grad_ref, 1)
 
-    group = share * n_z
-    for place in range(ring):
-        for e in range(2):
-            for i in range(share):
-                first = ((place // n_lat) * 2 + e) * n_lat * share + (place % n_lat) * share + i
-                for part in range(wide // LANES):
-                    blk[place, pl.ds(e * group + i * n_z, n_z), pl.ds(part * LANES, LANES)] = product[
-                        part, pl.ds(first, n_z, stride=ring * 2 * share), :
-                    ].astype(BF16)
-
-    def ring_copy(way, step):
-        lo, size = (0, 2 * group) if step else (way * group, group)
-        return remote(
-            ysend.at[way, step, pl.ds(lo, size), :],
-            yrecv.at[way, step, pl.ds(lo, size), :],
-            y_s.at[way, step],
-            y_r.at[way, step],
-            on_ring(ring_next if way == 0 else ring_prev),
-        )
-
-    for step in range(steps):
-        for way in range(2):
-            distance = steps - step
-            place = lax.rem(y + (distance if way == 0 else ring - distance), ring)
-            if step == 0:
-                lo = way * group
-                ysend[way, step, pl.ds(lo, group), :] = blk[place, pl.ds(lo, group), :]
-            else:
-                ring_copy(way, step - 1).wait_recv()
-                if step == 1:
-                    lo, rest = way * group, (1 - way) * group
-                    ysend[way, step, pl.ds(lo, group), :] = (
-                        blk[place, pl.ds(lo, group), :].astype(F32)
-                        + yrecv[way, 0, pl.ds(lo, group), :].astype(F32)
-                    ).astype(BF16)
-                    ysend[way, step, pl.ds(rest, group), :] = blk[place, pl.ds(rest, group), :]
-                else:
-                    ysend[way, step] = (
-                        blk[place].astype(F32) + yrecv[way, step - 1].astype(F32)
-                    ).astype(BF16)
-            ring_copy(way, step).start()
+    pl.when(jnp.logical_not(is_first))(ring_begin)
+    for way in range(2):
+        ring_step(1, way, way)
+    for step in range(2, steps):
+        for half_turn in range(2):
+            for way in range(2):
+                ring_step(step, way, way if half_turn else 1 - way)
     summed = blk[y].astype(F32)
     for way in range(2):
-        ring_copy(way, steps - 1).wait_recv()
+        for e in range(2):
+            ring_copy(way, steps - 1, e).wait_recv()
         summed = summed + yrecv[way, steps - 1].astype(F32)
     for part in range(wide // LANES):
         acc[part] = summed[:, part * LANES : (part + 1) * LANES]
@@ -627,11 +658,11 @@
 
     @pl.when(is_first)
     def _():
-        regroup_sent(in_ref, xp, 0)
+        regroup_sent(in_ref, raw.at[0], 0)
 
     @pl.when(is_last)
     def _():
-        regroup_sent(cot_ref, gown, 1)
+        regroup_sent(cot_ref, raw.at[1], 1)
 
     @pl.when(jnp.logical_not(is_last))
     def _():
@@ -648,7 +679,9 @@
     last.wait_send()
     for step in range(steps):
         for way in range(2):
-            ring_copy(way, step).wait_send()
+            for e in range(2):
+                if step or e == way:
+                    ring_copy(way, step, e).wait_send()
     for shift in range(1, n_z):
         z_copy(shift).wait_send()
 
@@ -665,14 +698,8 @@
     wide = channels // 2
     scale = 1.0 / math.sqrt(members * rows * n_lat * half * n_lon)
 
-    def padded(table):
-        table = table.astype(F32)
-        return jnp.pad(table, ((REACH, 16 - REACH), (0, LANES - table.shape[1])))
-
-    by_basis = jnp.transpose(basis_values, (0, 2, 1)).reshape(rows * n_lat, BASIS * TAPS)
-    table = jnp.concatenate([padded(lat_step), padded(lon_step), padded(by_basis)], axis=1)
-    constants = [jnp.asarray(t) for t in static_tables(rows, cols, half)]
     vmem = pl.BlockSpec(memory_space=pltpu.VMEM)
+    hbm = pl.BlockSpec(memory_space=pltpu.HBM)
     dma = pltpu.SemaphoreType.DMA
     section_out, section_grad, weight_grad = pl.pallas_call(
         functools.partial(step_kernel, (n_seg, n_lat, n_z, scale)),
@@ -681,9 +708,15 @@
             jax.ShapeDtypeStruct((2, rows * half, channels), BF16),
             jax.ShapeDtypeStruct((share, channels), F32),
         ),
-        in_specs=[vmem] * 9,
-        out_specs=(vmem, vmem, vmem),
+        in_specs=[hbm] * 6,
+        out_specs=(hbm, hbm, vmem),
         scratch_shapes=[
+            pltpu.VMEM((TAPS, rows * n_lat), jnp.int32),
+            pltpu.VMEM((TAPS, rows * n_lat), jnp.int32),
+            pltpu.VMEM((TAPS, BASIS, rows * n_lat), F32),
+            pltpu.VMEM((BASIS, channels, channels), BF16),
+            pltpu.VMEM((2, 2, rows, half, channels), BF16),
+            pltpu.VMEM((own, own), BF16),
             pltpu.VMEM((spots, channels), BF16),
             pltpu.VMEM((spots, channels), BF16),
             pltpu.VMEM((own, channels), BF16),
@@ -716,20 +749,23 @@
             dma((2, 2)),
             dma((3,)),
             dma((3,)),
-            dma((2, n_lat)),
-            dma((2, n_lat)),
+            dma((2, n_lat, 2)),
+            dma((2, n_lat, 2)),
             dma((n_z,)),
             dma((n_z,)),
+            dma((4,)),
         ],
         compiler_params=pltpu.CompilerParams(
-            collective_id=0, has_side_effects=True, vmem_limit_bytes=48 * 1024 * 1024
+            collective_id=0, has_side_effects=True, vmem_limit_bytes=67043328
+
         ),
         name="section_step",
     )(
-        table,
-        *constants,
-        inputs.reshape(members, rows * half, channels),
-        cotangent.reshape(members, rows * half, channels),
+        jnp.transpose(lat_step),
+        jnp.transpose(lon_step),
+        jnp.transpose(basis_values, (1, 2, 0)),
+        inputs,
+        cotangent,
         weights[0],
     )
     block = (1,) + inputs.shape

time: 134 us -> 123 us (0.918)
  local copies, waits for them, and re-layouts: 10.1 us -> 4.52 us
  Pallas kernels: 121 us -> 117 us
  other arithmetic: 1.41 us -> 0 us
    unnamed x13 -> x1, local copies, waits for them, and re-layouts: 5.86 us -> 1.33 us
    pallas_call x1, Pallas kernels: 121 us -> 117 us  [per_device(): pl.pallas_call(functools.partial(step_kernel, (n_seg, n_lat, n_z, scale))...]
    reshape x4 -> x0, local copies, waits for them, and re-layouts: 1.98 us -> none  [the longest x1 0.94 us: per_device(): inputs.reshape(members, rows * half, channels)]
    convert_element_type x2 -> x0, other arithmetic: 1.4 us -> none  [padded(): table = table.astype(F32)]
where the time goes in v2:
time: 123 us; the launch traced here: 122 us
  Pallas kernels  117 us (95%)
  local copies, waits for them, and re-layouts  4.52 us (4%)
    pallas_call x1, Pallas kernels, per_device(): pl.pallas_call(functools.partial(step_kernel, (n_seg, n_lat, n_z, scale))...  117 us

profile of v2, /device:TPU:1, one launch (start us, length us, event | category | flops | bytes accessed | tf_op | source)
XLA Modules:
  0.0 122.4 jit_solution(5502750246686419763)
XLA Ops:
  0.6 117.3 %section_step.1 = (bf16[2,64,512]{2,1,0:T(8,128)(2,1)}, bf16[2,64,512]{2,1,0:T(8,128)(2,1)}, f32[6,512]{1,0:T(8,128)}) custom-call(s32[9,64]{1,0:T(8,128)} %bitcast.11, s32[9,64]{1,0:T(8,128)} %bitcast.12, f32[9,3,64]{2,1,0:T(4,128)} %bitcast.8, bf16[2,16,4,512]{3,2,1,0:T(4,128)(2,1)} %in_ref.1, bf16[2,16,4,512]{3,2,1,0:T(4,128)(2,1)} %cot_ref.1, ...), custom_call_target="tpu_custom_call" | custom-call | tf_op jit(solution)/shard_map/section_step/pallas_call | solution.py:704
  117.9 1.6 %reshape.15 = bf16[1,2,16,4,512]{4,3,2,1,0:T(4,128)(2,1)} reshape(bf16[2,64,512]{2,1,0:T(8,128)(2,1)} %get-tuple-element.6) | data formatting | bytes 262144 | tf_op jit(solution)/shard_map/reshape | solution.py:773
  119.5 1.3 %copy.9 = f32[1,1,6,512]{3,1,2,0:T(1,128)} copy(f32[1,1,6,512]{3,2,1,0:T(8,128)} %bitcast.9) | data formatting | bytes 24576
  120.8 1.6 %reshape.16 = bf16[1,2,16,4,512]{4,3,2,1,0:T(4,128)(2,1)} reshape(bf16[2,64,512]{2,1,0:T(8,128)(2,1)} %get-tuple-element.7) | data formatting | bytes 262144 | tf_op jit(solution)/shard_map/reshape | solution.py:774

commit v3 on v2

--- a/solution.py
+++ b/solution.py
@@ -90,12 +90,12 @@
     lat_ref,
     lon_ref,
     basis_ref,
-    w_ref,
+    w_all,
     raw,
     pick,
     xp,
     gp,
-    gown,
+    grad,
     hb,
     ahead,
     back,
@@ -103,8 +103,6 @@
     spread_other,
     gate_other,
     slope,
-    ob,
-    gb,
     feat,
     product,
     blk,
@@ -117,8 +115,12 @@
     frecv,
     cin_s,
     cin_r,
-    hop_s,
-    hop_r,
+    own_s,
+    own_r,
+    far_s,
+    far_r,
+    swap_s,
+    swap_r,
     halo_s,
     halo_r,
     oc_s,
@@ -160,8 +162,9 @@
 
     has_up = lat > 0
     has_down = lat < n_lat - 1
-    is_first = seg == 0
-    is_last = seg == n_seg - 1
+    seg_next = lax.rem(seg + 1, n_seg)
+    seg_prev = lax.rem(seg + n_seg - 1, n_seg)
+    seg_far = lax.rem(seg + 2, n_seg)
     matched = core == member
 
     base = 4 * rows
@@ -191,7 +194,7 @@
 
     partner = at(z, member, 1 - core, lat)
 
-    fetch = pltpu.make_async_copy(w_hbm, w_ref, w_sem.at[0])
+    fetch = pltpu.make_async_copy(w_hbm, w_all.at[seg], w_sem.at[0])
     tables = [
         pltpu.make_async_copy(table_hbm, table_ref, w_sem.at[1 + number])
         for number, (table_hbm, table_ref) in enumerate(
@@ -231,18 +234,12 @@
         def _():
             greet(at(z, core, other, lat))
 
-    @pl.when(jnp.logical_not(is_first))
-    def _():
-        greet(at(z, member, core, lat, seg - 1))
-
-    @pl.when(jnp.logical_not(is_last))
-    def _():
-        greet(at(z, member, core, lat, seg + 1))
-
-    met = (n_z - 1) + 3 + 2 + 4
+    greet(at(z, member, core, lat, seg_next))
+    greet(at(z, member, core, lat, seg_prev))
+
+    met = (n_z - 1) + 3 + 2 + 4 + 2
     met = met + jnp.where(has_up, 3, 0) + jnp.where(has_down, 3, 0)
     met = met - jnp.where(matched, 2, 0)
-    met = met + jnp.where(is_first, 0, 1) + jnp.where(is_last, 0, 1)
     pl.semaphore_wait(barrier, met)
 
     def remote(src, dst, send_sem, recv_sem, device):
@@ -311,15 +308,78 @@
                     partner,
                 ).wait_send()
 
-    @pl.when(is_first)
-    def _():
-        regroup(in_ref, raw.at[0], 0)
-
-    @pl.when(is_last)
-    def _():
-        regroup(cot_ref, raw.at[1], 1)
-
-    for buffer in (xp, gp):
+    regroup(in_ref, raw.at[0], 0)
+
+    n_pieces = 2 * BASIS
+    part_rows = channels // 4
+    orders = (tuple(range(n_pieces)), tuple((k + BASIS) % n_pieces for k in range(n_pieces)))
+
+    def piece(weights, k, of_core):
+        start = pl.multiple_of(of_core * (channels // 2) + (k % 2) * part_rows, part_rows)
+        return weights.at[k // 2, pl.ds(start, part_rows), :]
+
+    def own_copy(way, k):
+        return remote(
+            piece(w_hbm, k, core),
+            piece(w_all.at[seg], k, core),
+            own_s.at[way, k],
+            own_r.at[way, k],
+            at(z, member, core, lat, seg_prev if way else seg_next),
+        )
+
+    def own_landed(way, k):
+        section = seg_next if way else seg_prev
+        landing = piece(w_all.at[section], k, core)
+        remote(landing, landing, own_s.at[way, k], own_r.at[way, k], partner).wait_recv()
+
+    def far_copy(way, k):
+        moved = piece(w_all.at[seg_next if way else seg_prev], k, core)
+        return remote(
+            moved,
+            moved,
+            far_s.at[k],
+            far_r.at[k],
+            at(z, member, core, lat, seg_prev if way else seg_next),
+        )
+
+    def far_landed(k):
+        landing = piece(w_all.at[seg_far], k, core)
+        remote(landing, landing, far_s.at[k], far_r.at[k], partner).wait_recv()
+
+    def swap_copy(which, k):
+        moved = piece(w_all.at[(seg_prev, seg_next, seg_far)[which]], k, core)
+        return remote(moved, moved, swap_s.at[which, k], swap_r.at[which, k], partner)
+
+    def swap_landed(which, k):
+        landing = piece(w_all.at[(seg_prev, seg_next, seg_far)[which]], k, 1 - core)
+        remote(landing, landing, swap_s.at[which, k], swap_r.at[which, k], partner).wait_recv()
+
+    for step in range(n_pieces):
+        for way in range(2):
+            own_copy(way, orders[way][step]).start()
+
+    def pump_near():
+        for step in range(n_pieces):
+            for way in range(2):
+                k = orders[way][step]
+                own_landed(way, k)
+                swap_copy(way, k).start()
+                if step < BASIS:
+                    far_copy(way, k).start()
+        for step in range(n_pieces):
+            for way in range(2):
+                swap_landed(way, orders[way][step])
+
+    def pump_far():
+        for step in range(BASIS):
+            for way in range(2):
+                k = orders[way][step]
+                far_landed(k)
+                swap_copy(2, k).start()
+        for k in range(n_pieces):
+            swap_landed(2, k)
+
+    for buffer in [xp.at[s] for s in range(n_seg)] + [gp.at[s] for s in range(n_seg)]:
 
         @pl.when(jnp.logical_not(has_up))
         def _():
@@ -480,74 +540,91 @@
             def _():
                 restore_copy(block, output, which, 0, origin).wait_recv()
 
-    def hop_ahead():
-        return remote(
-            ob, xp.at[pl.ds(0, own), :], hop_s.at[0], hop_r.at[0], at(z, member, core, lat, seg + 1)
-        )
-
-    def hop_back():
-        return remote(
-            gb, gown, hop_s.at[1], hop_r.at[1], at(z, member, core, lat, seg - 1)
-        )
-
-    @pl.when(is_first)
+    pair_spread = remote(spread.at[seg], spread_other, pair_s.at[0], pair_r.at[0], partner)
+
+    def forward(section):
+        halo_arrived(xp.at[section], section)
+        widened = xp[section]
+        mixed = None
+        for b in range(BASIS):
+            picked = jnp.dot(
+                ahead[pl.ds(b * own, own), :], widened, preferred_element_type=F32
+            ).astype(BF16)
+            spread[section, pl.ds(b * own, own), :] = picked
+            term = jnp.dot(picked, w_all[section, b], preferred_element_type=F32)
+            mixed = term if mixed is None else mixed + term
+        sigma = 1.0 / (1.0 + jnp.exp(-mixed))
+        result = (xp[section, pl.ds(0, own), :].astype(F32) + mixed * sigma).astype(BF16)
+        xp[section + 1, pl.ds(0, own), :] = result
+        if section + 1 < n_seg:
+            halo_start(result, xp.at[section + 1], section + 1)
+        slope[section] = sigma * (1.0 + mixed * (1.0 - sigma))
+
+        @pl.when(seg == section)
+        def _():
+            restore_start(xp.at[section + 1], out_ref, 0)
+            pair_spread.start()
+
+    regroup_arrived(in_ref, raw.at[0], 0)
+    xp[0, pl.ds(0, own), :] = raw[0].reshape(own, channels)
+    halo_start(xp[0, pl.ds(0, own), :], xp.at[0], 0)
+    regroup(cot_ref, raw.at[1], 1)
+    fetch.wait()
+
+    @pl.when(seg == 0)
     def _():
-        regroup_arrived(in_ref, raw.at[0], 0)
-        xp[pl.ds(0, own), :] = raw[0].reshape(own, channels)
-
-    @pl.when(jnp.logical_not(is_first))
+        forward(0)
+
+    pump_near()
+    pl.when(seg_far == 0)(pump_far)
+
+    @pl.when(seg != 0)
     def _():
-        hop_ahead().wait_recv()
-
-    halo_start(xp[pl.ds(0, own), :], xp, 0)
-    halo_arrived(xp, 0)
-    widened = xp[...]
-    for b in range(BASIS):
-        spread[pl.ds(b * own, own), :] = jnp.dot(
-            ahead[pl.ds(b * own, own), :], widened, preferred_element_type=F32
-        ).astype(BF16)
-    fetch.wait()
-    mixed = jnp.dot(spread[pl.ds(0, own), :], w_ref[0], preferred_element_type=F32)
-    for b in range(1, BASIS):
-        mixed = mixed + jnp.dot(
-            spread[pl.ds(b * own, own), :], w_ref[b], preferred_element_type=F32
-        )
-    sigma = 1.0 / (1.0 + jnp.exp(-mixed))
-    ob[...] = (xp[pl.ds(0, own), :].astype(F32) + mixed * sigma).astype(BF16)
-
-    @pl.when(jnp.logical_not(is_last))
-    def _():
-        hop_ahead().start()
-
-    slope[...] = sigma * (1.0 + mixed * (1.0 - sigma))
-    restore_start(ob, out_ref, 0)
-    pair_spread = remote(spread, spread_other, pair_s.at[0], pair_r.at[0], partner)
-    pair_spread.start()
-
-    @pl.when(is_last)
-    def _():
-        regroup_arrived(cot_ref, raw.at[1], 1)
-        gown[...] = raw[1].reshape(own, channels)
-
-    @pl.when(jnp.logical_not(is_last))
-    def _():
-        hop_back().wait_recv()
-
-    gate = (gown[...].astype(F32) * slope[...]).astype(BF16)
-    gp[pl.ds(0, own), :] = gate
-    halo_start(gate, gp, 1)
-    pair_gate = remote(gp.at[pl.ds(0, own), :], gate_other, pair_s.at[1], pair_r.at[1], partner)
+        forward(0)
+
+    for section in range(1, n_seg):
+        pl.when(seg_far == section)(pump_far)
+        forward(section)
+
+    regroup_arrived(cot_ref, raw.at[1], 1)
+    grad[...] = raw[1].reshape(own, channels)
+
+    def open_gate(section):
+        gate = (grad[...].astype(F32) * slope[section]).astype(BF16)
+        gp[section, pl.ds(0, own), :] = gate
+        halo_start(gate, gp.at[section], n_seg + section)
+
+    def pull(section):
+        halo_arrived(gp.at[section], n_seg + section)
+        for b in range(BASIS):
+            feat[pl.ds(b * spots, spots), :] = lax.dot_general(
+                gp[section], w_all[section, b], (((1,), (1,)), ((), ())), preferred_element_type=F32
+            ).astype(BF16)
+        pulled = jnp.dot(back[...], feat[...], preferred_element_type=F32)
+        grad[...] = (grad[...].astype(F32) + pulled).astype(BF16)
+
+    for section in range(n_seg - 1, 0, -1):
+
+        @pl.when(seg < section)
+        def _():
+            open_gate(section)
+            pull(section)
+
+    open_gate(seg)
+    pair_gate = remote(
+        gp.at[seg, pl.ds(0, own), :], gate_other, pair_s.at[1], pair_r.at[1], partner
+    )
     pair_gate.start()
     pair_spread.wait_recv()
     pair_gate.wait_recv()
 
     columns = pl.ds(pl.multiple_of(core * wide, wide), wide)
     gate_both = jnp.concatenate(
-        [gp[pl.ds(0, own), columns], gate_other[:, columns]], axis=0
+        [gp[seg, pl.ds(0, own), columns], gate_other[:, columns]], axis=0
     )
     for b in range(BASIS):
         both = jnp.concatenate(
-            [spread[pl.ds(b * own, own), :], spread_other[pl.ds(b * own, own), :]], axis=0
+            [spread[seg, pl.ds(b * own, own), :], spread_other[pl.ds(b * own, own), :]], axis=0
         )
         term = scale * lax.dot_general(
             both, gate_both, (((0,), (0,)), ((), ())), preferred_element_type=F32
@@ -593,23 +670,10 @@
         for way in range(2):
             ring_step(1, way, 1 - way)
 
-    pl.when(is_first)(ring_begin)
-
-    halo_arrived(gp, 1)
-    for b in range(BASIS):
-        feat[pl.ds(b * spots, spots), :] = lax.dot_general(
-            gp[...], w_ref[b], (((1,), (1,)), ((), ())), preferred_element_type=F32
-        ).astype(BF16)
-    pulled = jnp.dot(back[...], feat[...], preferred_element_type=F32)
-    gb[...] = (gown[...].astype(F32) + pulled).astype(BF16)
-
-    @pl.when(jnp.logical_not(is_first))
-    def _():
-        hop_back().start()
-
-    restore_start(gb, grad_ref, 1)
-
-    pl.when(jnp.logical_not(is_first))(ring_begin)
+    ring_begin()
+    pull(seg)
+    restore_start(grad, grad_ref, 1)
+
     for way in range(2):
         ring_step(1, way, way)
     for step in range(2, steps):
@@ -653,27 +717,23 @@
     wg_ref[:, :wide] = jnp.where(core == 0, mine, theirs)
     wg_ref[:, wide:] = jnp.where(core == 0, theirs, mine)
 
-    restore_finish(ob, out_ref, 0)
-    restore_finish(gb, grad_ref, 1)
-
-    @pl.when(is_first)
-    def _():
-        regroup_sent(in_ref, raw.at[0], 0)
-
-    @pl.when(is_last)
-    def _():
-        regroup_sent(cot_ref, raw.at[1], 1)
-
-    @pl.when(jnp.logical_not(is_last))
-    def _():
-        hop_ahead().wait_send()
-
-    @pl.when(jnp.logical_not(is_first))
-    def _():
-        hop_back().wait_send()
-
-    halo_sent(xp, 0)
-    halo_sent(gp, 1)
+    restore_finish(xp.at[seg + 1], out_ref, 0)
+    restore_finish(grad, grad_ref, 1)
+    regroup_sent(in_ref, raw.at[0], 0)
+    regroup_sent(cot_ref, raw.at[1], 1)
+    for k in range(n_pieces):
+        for way in range(2):
+            own_copy(way, k).wait_send()
+        far_copy(k // BASIS, k).wait_send()
+        for which in range(3):
+            swap_copy(which, k).wait_send()
+    for section in range(n_seg):
+        halo_sent(xp.at[section], section)
+
+        @pl.when(seg <= section)
+        def _():
+            halo_sent(gp.at[section], n_seg + section)
+
     pair_spread.wait_send()
     pair_gate.wait_send()
     last.wait_send()
@@ -709,26 +769,24 @@
             jax.ShapeDtypeStruct((share, channels), F32),
         ),
         in_specs=[hbm] * 6,
-        out_specs=(hbm, hbm, vmem),
+        out_specs=(vmem, vmem, vmem),
         scratch_shapes=[
             pltpu.VMEM((TAPS, rows * n_lat), jnp.int32),
             pltpu.VMEM((TAPS, rows * n_lat), jnp.int32),
             pltpu.VMEM((TAPS, BASIS, rows * n_lat), F32),
-            pltpu.VMEM((BASIS, channels, channels), BF16),
+            pltpu.VMEM((n_seg, BASIS, channels, channels), BF16),
             pltpu.VMEM((2, 2, rows, half, channels), BF16),
             pltpu.VMEM((own, own), BF16),
-            pltpu.VMEM((spots, channels), BF16),
-            pltpu.VMEM((spots, channels), BF16),
+            pltpu.VMEM((n_seg + 1, spots, channels), BF16),
+            pltpu.VMEM((n_seg, spots, channels), BF16),
             pltpu.VMEM((own, channels), BF16),
-            pltpu.VMEM((2, own, channels), BF16),
+            pltpu.VMEM((2 * n_seg, own, channels), BF16),
             pltpu.VMEM((BASIS * own, spots), BF16),
             pltpu.VMEM((own, BASIS * spots), BF16),
-            pltpu.VMEM((BASIS * own, channels), BF16),
+            pltpu.VMEM((n_seg, BASIS * own, channels), BF16),
             pltpu.VMEM((BASIS * own, channels), BF16),
             pltpu.VMEM((own, channels), BF16),
-            pltpu.VMEM((own, channels), F32),
-            pltpu.VMEM((own, channels), BF16),
-            pltpu.VMEM((own, channels), BF16),
+            pltpu.VMEM((n_seg, own, channels), F32),
             pltpu.VMEM((BASIS * spots, channels), BF16),
             pltpu.VMEM((wide // LANES, BASIS * channels, LANES), F32),
             pltpu.VMEM((ring, 2 * share * n_z, wide), BF16),
@@ -741,10 +799,14 @@
             pltpu.VMEM((-(-share // 8) * 8, wide), F32),
             dma((2, 2)),
             dma((2, 2)),
-            dma((2,)),
-            dma((2,)),
-            dma((2, 8)),
-            dma((2, 8)),
+            dma((2, 2 * BASIS)),
+            dma((2, 2 * BASIS)),
+            dma((2 * BASIS,)),
+            dma((2 * BASIS,)),
+            dma((3, 2 * BASIS)),
+            dma((3, 2 * BASIS)),
+            dma((2 * n_seg, 8)),
+            dma((2 * n_seg, 8)),
             dma((2, 2)),
             dma((2, 2)),
             dma((3,)),
@@ -756,17 +818,21 @@
             dma((4,)),
         ],
         compiler_params=pltpu.CompilerParams(
-            collective_id=0, has_side_effects=True, vmem_limit_bytes=67043328
-
+            collective_id=0, has_side_effects=True, vmem_limit_bytes=50331648
         ),
         name="section_step",
     )(
-        jnp.transpose(lat_step),
-        jnp.transpose(lon_step),
-        jnp.transpose(basis_values, (1, 2, 0)),
-        inputs,
-        cotangent,
-        weights[0],
+        *(
+            pltpu.with_memory_space_constraint(array, pltpu.HBM)
+            for array in (
+                jnp.transpose(lat_step),
+                jnp.transpose(lon_step),
+                jnp.transpose(basis_values, (1, 2, 0)),
+                inputs,
+                cotangent,
+                weights[0],
+            )
+        )
     )
     block = (1,) + inputs.shape
     return (

time: 123 us -> 107 us (0.87)
  Pallas kernels: 117 us -> 104 us
  local copies, waits for them, and re-layouts: 4.52 us -> 1.99 us
    pallas_call x1, Pallas kernels: 117 us -> 104 us  [per_device(): pl.pallas_call(functools.partial(step_kernel, (n_seg, n_lat, n_z, scale))...]
where the time goes in v3:
time: 107 us
  Pallas kernels  104 us (97%)
  local copies, waits for them, and re-layouts  1.99 us (2%)
    pallas_call x1, Pallas kernels, per_device(): pl.pallas_call(functools.partial(step_kernel, (n_seg, n_lat, n_z, scale))...  104 us

profile of v3, /device:TPU:1, one launch (start us, length us, event | category | flops | bytes accessed | tf_op | source)
XLA Modules:
  0.0 106.8 jit_solution(3985494226935697599)
XLA Ops:
  0.6 104.1 %section_step.1 = (bf16[2,64,512]{2,1,0:T(8,128)(2,1)S(1)}, bf16[2,64,512]{2,1,0:T(8,128)(2,1)S(1)}, f32[6,512]{1,0:T(8,128)S(1)}) custom-call(s32[9,64]{1,0:T(8,128)} %bitcast.11, s32[9,64]{1,0:T(8,128)} %bitcast.12, f32[9,3,64]{2,1,0:T(4,128)} %bitcast.9, bf16[2,16,4,512]{3,2,1,0:T(4,128)(2,1)} %in_ref.1, bf16[2,16,4,512]{3,2,1,0:T(4,128)(2,1)} %cot_ref.1, ...), custom_call_target="tpu_custom_call" | custom-call | tf_op jit(solution)/shard_map/section_step/pallas_call | solution.py:764
  104.8 0.7 reshape.15
  105.4 0.6 copy.9
  106.1 0.7 reshape.16

commit v4 on v3

--- a/solution.py
+++ b/solution.py
@@ -119,6 +119,8 @@
     own_r,
     far_s,
     far_r,
+    side_s,
+    side_r,
     swap_s,
     swap_r,
     halo_s,
@@ -311,29 +313,32 @@
     regroup(in_ref, raw.at[0], 0)
 
     n_pieces = 2 * BASIS
-    part_rows = channels // 4
+    part_rows = channels // 8
     orders = (tuple(range(n_pieces)), tuple((k + BASIS) % n_pieces for k in range(n_pieces)))
-
-    def piece(weights, k, of_core):
-        start = pl.multiple_of(of_core * (channels // 2) + (k % 2) * part_rows, part_rows)
-        return weights.at[k // 2, pl.ds(start, part_rows), :]
+    sections = (seg_prev, seg_next, seg_far)
+    parity = lax.rem(z, 2)
+    z_next = at(lax.rem(z + 1, n_z), member, core, lat)
+    z_prev = at(lax.rem(z + n_z - 1, n_z), member, core, lat)
+
+    def piece(weights, k, of_parity, of_core):
+        start = (2 * of_parity + of_core) * (channels // 4) + (k % 2) * part_rows
+        return weights.at[k // 2, pl.ds(pl.multiple_of(start, part_rows), part_rows), :]
 
     def own_copy(way, k):
         return remote(
-            piece(w_hbm, k, core),
-            piece(w_all.at[seg], k, core),
+            piece(w_hbm, k, parity, core),
+            piece(w_all.at[seg], k, parity, core),
             own_s.at[way, k],
             own_r.at[way, k],
             at(z, member, core, lat, seg_prev if way else seg_next),
         )
 
     def own_landed(way, k):
-        section = seg_next if way else seg_prev
-        landing = piece(w_all.at[section], k, core)
+        landing = piece(w_all.at[sections[way]], k, parity, core)
         remote(landing, landing, own_s.at[way, k], own_r.at[way, k], partner).wait_recv()
 
     def far_copy(way, k):
-        moved = piece(w_all.at[seg_next if way else seg_prev], k, core)
+        moved = piece(w_all.at[sections[way]], k, parity, core)
         return remote(
             moved,
             moved,
@@ -343,41 +348,73 @@
         )
 
     def far_landed(k):
-        landing = piece(w_all.at[seg_far], k, core)
+        landing = piece(w_all.at[seg_far], k, parity, core)
         remote(landing, landing, far_s.at[k], far_r.at[k], partner).wait_recv()
 
-    def swap_copy(which, k):
-        moved = piece(w_all.at[(seg_prev, seg_next, seg_far)[which]], k, core)
-        return remote(moved, moved, swap_s.at[which, k], swap_r.at[which, k], partner)
-
-    def swap_landed(which, k):
-        landing = piece(w_all.at[(seg_prev, seg_next, seg_far)[which]], k, 1 - core)
-        remote(landing, landing, swap_s.at[which, k], swap_r.at[which, k], partner).wait_recv()
+    def side_copy(which, k):
+        moved = piece(w_all.at[sections[which]], k, parity, core)
+        return remote(
+            moved, moved, side_s.at[which, k], side_r.at[which, k], z_prev if k % 2 else z_next
+        )
+
+    def side_landed(which, k):
+        landing = piece(w_all.at[sections[which]], k, 1 - parity, core)
+        remote(landing, landing, side_s.at[which, k], side_r.at[which, k], partner).wait_recv()
+
+    def swap_copy(which, k, other):
+        moved = piece(w_all.at[sections[which]], k, 1 - parity if other else parity, core)
+        return remote(
+            moved, moved, swap_s.at[which, k, other], swap_r.at[which, k, other], partner
+        )
+
+    def swap_landed(which, k, other):
+        landing = piece(w_all.at[sections[which]], k, 1 - parity if other else parity, 1 - core)
+        remote(
+            landing, landing, swap_s.at[which, k, other], swap_r.at[which, k, other], partner
+        ).wait_recv()
 
     for step in range(n_pieces):
         for way in range(2):
             own_copy(way, orders[way][step]).start()
 
-    def pump_near():
+    def pump_near(first, last):
+        for step in range(first, last):
+            for way in range(2):
+                k = orders[way][step]
+                own_landed(way, k)
+                side_copy(way, k).start()
+                if step < BASIS:
+                    far_copy(way, k).start()
+                swap_copy(way, k, 0).start()
+
+    def finish_near():
         for step in range(n_pieces):
             for way in range(2):
                 k = orders[way][step]
-                own_landed(way, k)
-                swap_copy(way, k).start()
-                if step < BASIS:
-                    far_copy(way, k).start()
-        for step in range(n_pieces):
-            for way in range(2):
-                swap_landed(way, orders[way][step])
+                side_landed(way, k)
+                swap_copy(way, k, 1).start()
 
     def pump_far():
         for step in range(BASIS):
             for way in range(2):
                 k = orders[way][step]
                 far_landed(k)
-                swap_copy(2, k).start()
+                side_copy(2, k).start()
+                swap_copy(2, k, 0).start()
+
+    def near_landed():
+        for step in range(n_pieces):
+            for way in range(2):
+                for other in range(2):
+                    swap_landed(way, orders[way][step], other)
+
+    def finish_far():
         for k in range(n_pieces):
-            swap_landed(2, k)
+            side_landed(2, k)
+            swap_copy(2, k, 1).start()
+        for k in range(n_pieces):
+            for other in range(2):
+                swap_landed(2, k, other)
 
     for buffer in [xp.at[s] for s in range(n_seg)] + [gp.at[s] for s in range(n_seg)]:
 
@@ -565,25 +602,29 @@
             restore_start(xp.at[section + 1], out_ref, 0)
             pair_spread.start()
 
+    pump_near(0, 4)
     regroup_arrived(in_ref, raw.at[0], 0)
     xp[0, pl.ds(0, own), :] = raw[0].reshape(own, channels)
     halo_start(xp[0, pl.ds(0, own), :], xp.at[0], 0)
     regroup(cot_ref, raw.at[1], 1)
+    pump_near(4, n_pieces)
     fetch.wait()
 
     @pl.when(seg == 0)
     def _():
         forward(0)
 
-    pump_near()
-    pl.when(seg_far == 0)(pump_far)
+    finish_near()
+    pump_far()
+    near_landed()
+    pl.when(seg_far == 0)(finish_far)
 
     @pl.when(seg != 0)
     def _():
         forward(0)
 
     for section in range(1, n_seg):
-        pl.when(seg_far == section)(pump_far)
+        pl.when(seg_far == section)(finish_far)
         forward(section)
 
     regroup_arrived(cot_ref, raw.at[1], 1)
@@ -636,57 +677,65 @@
 
     group = share * n_z
 
-    def ring_copy(way, step, e):
+    parts = wide // LANES
+
+    def ring_copy(way, step, part, e):
         return remote(
-            ysend.at[way, step, pl.ds(e * group, group), :],
-            yrecv.at[way, step, pl.ds(e * group, group), :],
-            y_s.at[way, step, e],
-            y_r.at[way, step, e],
+            ysend.at[way, step, part, pl.ds(e * group, group), :],
+            yrecv.at[way, step, part, pl.ds(e * group, group), :],
+            y_s.at[way, step, part, e],
+            y_r.at[way, step, part, e],
             on_ring(ring_next if way == 0 else ring_prev),
         )
 
-    def ring_step(step, way, e):
+    def ring_step(step, way, part, e):
         distance = steps - step
         place = lax.rem(y + (distance if way == 0 else ring - distance), ring)
-        part = pl.ds(e * group, group)
-        term = blk[place, part, :]
+        span = pl.ds(e * group, group)
+        term = blk[part, place, span, :]
         if step > 1 or (step == 1 and e == way):
-            ring_copy(way, step - 1, e).wait_recv()
-            term = (term.astype(F32) + yrecv[way, step - 1, part, :].astype(F32)).astype(BF16)
-        ysend[way, step, part, :] = term
-        ring_copy(way, step, e).start()
+            ring_copy(way, step - 1, part, e).wait_recv()
+            term = (term.astype(F32) + yrecv[way, step - 1, part, span, :].astype(F32)).astype(
+                BF16
+            )
+        ysend[way, step, part, span, :] = term
+        ring_copy(way, step, part, e).start()
 
     def ring_begin():
-        for place in range(ring):
-            for e in range(2):
-                for i in range(share):
-                    first = ((place // n_lat) * 2 + e) * n_lat * share + (place % n_lat) * share + i
-                    for part in range(wide // LANES):
-                        blk[
-                            place, pl.ds(e * group + i * n_z, n_z), pl.ds(part * LANES, LANES)
-                        ] = product[part, pl.ds(first, n_z, stride=ring * 2 * share), :].astype(BF16)
-        for way in range(2):
-            ring_step(0, way, way)
-        for way in range(2):
-            ring_step(1, way, 1 - way)
+        for part in range(parts):
+            for place in range(ring):
+                for e in range(2):
+                    for i in range(share):
+                        first = ((place // n_lat) * 2 + e) * n_lat * share
+                        first = first + (place % n_lat) * share + i
+                        blk[part, place, pl.ds(e * group + i * n_z, n_z), :] = product[
+                            part, pl.ds(first, n_z, stride=ring * 2 * share), :
+                        ].astype(BF16)
+            for way in range(2):
+                ring_step(0, way, part, way)
+        for part in range(parts):
+            for way in range(2):
+                ring_step(1, way, part, 1 - way)
 
     ring_begin()
     pull(seg)
     restore_start(grad, grad_ref, 1)
 
-    for way in range(2):
-        ring_step(1, way, way)
+    for part in range(parts):
+        for way in range(2):
+            ring_step(1, way, part, way)
     for step in range(2, steps):
         for half_turn in range(2):
-            for way in range(2):
-                ring_step(step, way, way if half_turn else 1 - way)
-    summed = blk[y].astype(F32)
-    for way in range(2):
-        for e in range(2):
-            ring_copy(way, steps - 1, e).wait_recv()
-        summed = summed + yrecv[way, steps - 1].astype(F32)
-    for part in range(wide // LANES):
-        acc[part] = summed[:, part * LANES : (part + 1) * LANES]
+            for part in range(parts):
+                for way in range(2):
+                    ring_step(step, way, part, way if half_turn else 1 - way)
+    for part in range(parts):
+        summed = blk[part, y].astype(F32)
+        for way in range(2):
+            for e in range(2):
+                ring_copy(way, steps - 1, part, e).wait_recv()
+            summed = summed + yrecv[way, steps - 1, part].astype(F32)
+        acc[pl.ds(part * 2 * group, 2 * group), :] = summed
 
     def z_copy(shift):
         to = lax.rem(z + shift, n_z)
@@ -694,22 +743,30 @@
             zsend.at[to], zrecv.at[z], z_s.at[shift], z_r.at[shift], at(to, member, core, lat)
         )
 
+    slab = parts * 2 * share
     for to in range(n_z):
-        for part in range(wide // LANES):
-            zsend[to, pl.ds(0, 2 * share), pl.ds(part * LANES, LANES)] = acc[
-                part, pl.ds(to, 2 * share, stride=n_z), :
-            ].astype(BF16)
+        zsend[to] = acc[pl.ds(to, slab, stride=n_z), :].astype(BF16)
     for shift in range(1, n_z):
         z_copy(shift).start()
-    total = zsend[z][: 2 * share].astype(F32)
+    total = zsend[z].astype(F32)
     for shift in range(1, n_z):
         from_z = lax.rem(z + n_z - shift, n_z)
         remote(
             zsend.at[0], zrecv.at[from_z], z_s.at[shift], z_r.at[shift], partner
         ).wait_recv()
-        total = total + zrecv[from_z][: 2 * share].astype(F32)
-    mine = jnp.where(core == 0, total[:share], total[share:])
-    fsend[pl.ds(0, share), :] = jnp.where(core == 0, total[share:], total[:share])
+        total = total + zrecv[from_z].astype(F32)
+
+    def rows_for(e):
+        return jnp.concatenate(
+            [
+                total[(2 * part + e) * share : (2 * part + e + 1) * share]
+                for part in range(parts)
+            ],
+            axis=1,
+        )
+
+    mine = jnp.where(core == 0, rows_for(0), rows_for(1))
+    fsend[pl.ds(0, share), :] = jnp.where(core == 0, rows_for(1), rows_for(0))
     last = remote(fsend, frecv, pair_s.at[2], pair_r.at[2], partner)
     last.start()
     last.wait_recv()
@@ -726,7 +783,9 @@
             own_copy(way, k).wait_send()
         far_copy(k // BASIS, k).wait_send()
         for which in range(3):
-            swap_copy(which, k).wait_send()
+            side_copy(which, k).wait_send()
+            for other in range(2):
+                swap_copy(which, k, other).wait_send()
     for section in range(n_seg):
         halo_sent(xp.at[section], section)
 
@@ -739,9 +798,10 @@
     last.wait_send()
     for step in range(steps):
         for way in range(2):
-            for e in range(2):
-                if step or e == way:
-                    ring_copy(way, step, e).wait_send()
+            for part in range(parts):
+                for e in range(2):
+                    if step or e == way:
+                        ring_copy(way, step, part, e).wait_send()
     for shift in range(1, n_z):
         z_copy(shift).wait_send()
 
@@ -756,6 +816,7 @@
     ring = 2 * n_lat
     share = BASIS * channels // (n_lon * n_lat)
     wide = channels // 2
+    parts = wide // LANES
     scale = 1.0 / math.sqrt(members * rows * n_lat * half * n_lon)
 
     vmem = pl.BlockSpec(memory_space=pltpu.VMEM)
@@ -789,12 +850,12 @@
             pltpu.VMEM((n_seg, own, channels), F32),
             pltpu.VMEM((BASIS * spots, channels), BF16),
             pltpu.VMEM((wide // LANES, BASIS * channels, LANES), F32),
-            pltpu.VMEM((ring, 2 * share * n_z, wide), BF16),
-            pltpu.VMEM((2, n_lat, 2 * share * n_z, wide), BF16),
-            pltpu.VMEM((2, n_lat, 2 * share * n_z, wide), BF16),
-            pltpu.VMEM((wide // LANES, 2 * share * n_z, LANES), F32),
-            pltpu.VMEM((n_z, -(-2 * share // 16) * 16, wide), BF16),
-            pltpu.VMEM((n_z, -(-2 * share // 16) * 16, wide), BF16),
+            pltpu.VMEM((parts, ring, 2 * share * n_z, LANES), BF16),
+            pltpu.VMEM((2, n_lat, parts, 2 * share * n_z, LANES), BF16),
+            pltpu.VMEM((2, n_lat, parts, 2 * share * n_z, LANES), BF16),
+            pltpu.VMEM((parts * 2 * share * n_z, LANES), F32),
+            pltpu.VMEM((n_z, parts * 2 * share, LANES), BF16),
+            pltpu.VMEM((n_z, parts * 2 * share, LANES), BF16),
             pltpu.VMEM((-(-share // 8) * 8, wide), F32),
             pltpu.VMEM((-(-share // 8) * 8, wide), F32),
             dma((2, 2)),
@@ -805,14 +866,16 @@
             dma((2 * BASIS,)),
             dma((3, 2 * BASIS)),
             dma((3, 2 * BASIS)),
+            dma((3, 2 * BASIS, 2)),
+            dma((3, 2 * BASIS, 2)),
             dma((2 * n_seg, 8)),
             dma((2 * n_seg, 8)),
             dma((2, 2)),
             dma((2, 2)),
             dma((3,)),
             dma((3,)),
-            dma((2, n_lat, 2)),
-            dma((2, n_lat, 2)),
+            dma((2, n_lat, parts, 2)),
+            dma((2, n_lat, parts, 2)),
             dma((n_z,)),
             dma((n_z,)),
             dma((4,)),

time: 107 us -> 100 us (0.935)
  Pallas kernels: 104 us -> 97.2 us
    pallas_call x1, Pallas kernels: 104 us -> 97.2 us  [per_device(): pl.pallas_call(functools.partial(step_kernel, (n_seg, n_lat, n_z, scale))...]
where the time goes in v4:
time: 100 us; the launch traced here: 99.9 us
  Pallas kernels  97.2 us (97%)
  local copies, waits for them, and re-layouts  1.99 us (2%)
    pallas_call x1, Pallas kernels, per_device(): pl.pallas_call(functools.partial(step_kernel, (n_seg, n_lat, n_z, scale))...  97.2 us

profile of v4, /device:TPU:1, one launch (start us, length us, event | category | flops | bytes accessed | tf_op | source)
XLA Modules:
  0.0 99.9 jit_solution(5046044395923002150)
XLA Ops:
  0.6 97.2 %section_step.1 = (bf16[2,64,512]{2,1,0:T(8,128)(2,1)S(1)}, bf16[2,64,512]{2,1,0:T(8,128)(2,1)S(1)}, f32[6,512]{1,0:T(8,128)S(1)}) custom-call(s32[9,64]{1,0:T(8,128)} %bitcast.11, s32[9,64]{1,0:T(8,128)} %bitcast.12, f32[9,3,64]{2,1,0:T(4,128)} %bitcast.9, bf16[2,16,4,512]{3,2,1,0:T(4,128)(2,1)} %in_ref.1, bf16[2,16,4,512]{3,2,1,0:T(4,128)(2,1)} %cot_ref.1, ...), custom_call_target="tpu_custom_call" | custom-call | tf_op jit(solution)/shard_map/section_step/pallas_call | solution.py:825
  97.9 0.7 reshape.15
  98.6 0.6 copy.9
  99.2 0.7 reshape.16

commit v5 on v4

--- a/solution.py
+++ b/solution.py
@@ -316,9 +316,17 @@
     part_rows = channels // 8
     orders = (tuple(range(n_pieces)), tuple((k + BASIS) % n_pieces for k in range(n_pieces)))
     sections = (seg_prev, seg_next, seg_far)
-    parity = lax.rem(z, 2)
-    z_next = at(lax.rem(z + 1, n_z), member, core, lat)
-    z_prev = at(lax.rem(z + n_z - 1, n_z), member, core, lat)
+    parities = (lax.rem(y, 2), lax.rem(z, 2))
+    sides = (
+        (on_ring(ring_next), on_ring(ring_prev)),
+        (
+            at(lax.rem(z + 1, n_z), member, core, lat),
+            at(lax.rem(z + n_z - 1, n_z), member, core, lat),
+        ),
+    )
+
+    def axis_of(which, k):
+        return which if which < 2 else k // BASIS
 
     def piece(weights, k, of_parity, of_core):
         start = (2 * of_parity + of_core) * (channels // 4) + (k % 2) * part_rows
@@ -326,19 +334,19 @@
 
     def own_copy(way, k):
         return remote(
-            piece(w_hbm, k, parity, core),
-            piece(w_all.at[seg], k, parity, core),
+            piece(w_hbm, k, parities[way], core),
+            piece(w_all.at[seg], k, parities[way], core),
             own_s.at[way, k],
             own_r.at[way, k],
             at(z, member, core, lat, seg_prev if way else seg_next),
         )
 
     def own_landed(way, k):
-        landing = piece(w_all.at[sections[way]], k, parity, core)
+        landing = piece(w_all.at[sections[way]], k, parities[way], core)
         remote(landing, landing, own_s.at[way, k], own_r.at[way, k], partner).wait_recv()
 
     def far_copy(way, k):
-        moved = piece(w_all.at[sections[way]], k, parity, core)
+        moved = piece(w_all.at[sections[way]], k, parities[way], core)
         return remote(
             moved,
             moved,
@@ -348,27 +356,32 @@
         )
 
     def far_landed(k):
-        landing = piece(w_all.at[seg_far], k, parity, core)
+        landing = piece(w_all.at[seg_far], k, parities[axis_of(2, k)], core)
         remote(landing, landing, far_s.at[k], far_r.at[k], partner).wait_recv()
 
     def side_copy(which, k):
-        moved = piece(w_all.at[sections[which]], k, parity, core)
+        axis = axis_of(which, k)
+        moved = piece(w_all.at[sections[which]], k, parities[axis], core)
         return remote(
-            moved, moved, side_s.at[which, k], side_r.at[which, k], z_prev if k % 2 else z_next
+            moved, moved, side_s.at[which, k], side_r.at[which, k], sides[axis][k % 2]
         )
 
     def side_landed(which, k):
-        landing = piece(w_all.at[sections[which]], k, 1 - parity, core)
+        landing = piece(w_all.at[sections[which]], k, 1 - parities[axis_of(which, k)], core)
         remote(landing, landing, side_s.at[which, k], side_r.at[which, k], partner).wait_recv()
 
+    def swap_of(which, k, other, of_core):
+        parity = parities[axis_of(which, k)]
+        return piece(w_all.at[sections[which]], k, 1 - parity if other else parity, of_core)
+
     def swap_copy(which, k, other):
-        moved = piece(w_all.at[sections[which]], k, 1 - parity if other else parity, core)
+        moved = swap_of(which, k, other, core)
         return remote(
             moved, moved, swap_s.at[which, k, other], swap_r.at[which, k, other], partner
         )
 
     def swap_landed(which, k, other):
-        landing = piece(w_all.at[sections[which]], k, 1 - parity if other else parity, 1 - core)
+        landing = swap_of(which, k, other, 1 - core)
         remote(
             landing, landing, swap_s.at[which, k, other], swap_r.at[which, k, other], partner
         ).wait_recv()
@@ -377,22 +390,16 @@
         for way in range(2):
             own_copy(way, orders[way][step]).start()
 
-    def pump_near(first, last):
+    def pump_near(first, last, both):
         for step in range(first, last):
-            for way in range(2):
+            for way in (1, 0):
                 k = orders[way][step]
                 own_landed(way, k)
-                side_copy(way, k).start()
+                if way or both:
+                    side_copy(way, k).start()
                 if step < BASIS:
                     far_copy(way, k).start()
                 swap_copy(way, k, 0).start()
-
-    def finish_near():
-        for step in range(n_pieces):
-            for way in range(2):
-                k = orders[way][step]
-                side_landed(way, k)
-                swap_copy(way, k, 1).start()
 
     def pump_far():
         for step in range(BASIS):
@@ -402,19 +409,28 @@
                 side_copy(2, k).start()
                 swap_copy(2, k, 0).start()
 
-    def near_landed():
-        for step in range(n_pieces):
-            for way in range(2):
-                for other in range(2):
-                    swap_landed(way, orders[way][step], other)
-
-    def finish_far():
-        for k in range(n_pieces):
-            side_landed(2, k)
-            swap_copy(2, k, 1).start()
+    def sides_landed(which):
+        order = orders[which] if which < 2 else range(n_pieces)
+        for k in order:
+            side_landed(which, k)
+            swap_copy(which, k, 1).start()
+
+    def swaps_landed(which):
         for k in range(n_pieces):
             for other in range(2):
-                swap_landed(2, k, other)
+                swap_landed(which, k, other)
+
+    def weights_here(section):
+        @pl.when(seg_far == section)
+        def _():
+            sides_landed(2)
+            swaps_landed(2)
+
+        for which in range(2):
+
+            @pl.when(sections[which] == section)
+            def _():
+                swaps_landed(which)
 
     for buffer in [xp.at[s] for s in range(n_seg)] + [gp.at[s] for s in range(n_seg)]:
 
@@ -602,29 +618,32 @@
             restore_start(xp.at[section + 1], out_ref, 0)
             pair_spread.start()
 
-    pump_near(0, 4)
+    early = 4
+    pump_near(0, early, False)
     regroup_arrived(in_ref, raw.at[0], 0)
     xp[0, pl.ds(0, own), :] = raw[0].reshape(own, channels)
     halo_start(xp[0, pl.ds(0, own), :], xp.at[0], 0)
-    regroup(cot_ref, raw.at[1], 1)
-    pump_near(4, n_pieces)
+    for step in range(early):
+        side_copy(0, orders[0][step]).start()
+    pump_near(early, n_pieces, True)
     fetch.wait()
 
     @pl.when(seg == 0)
     def _():
         forward(0)
 
-    finish_near()
+    sides_landed(1)
     pump_far()
-    near_landed()
-    pl.when(seg_far == 0)(finish_far)
+    sides_landed(0)
 
     @pl.when(seg != 0)
     def _():
+        weights_here(0)
         forward(0)
 
+    regroup(cot_ref, raw.at[1], 1)
     for section in range(1, n_seg):
-        pl.when(seg_far == section)(finish_far)
+        weights_here(section)
         forward(section)
 
     regroup_arrived(cot_ref, raw.at[1], 1)

time: 100 us -> 101 us (1.010)
  no operation moved by 1% of the time
where the time goes in v5:
time: 101 us
  Pallas kernels  97.9 us (97%)
  local copies, waits for them, and re-layouts  1.99 us (2%)
    pallas_call x1, Pallas kernels, per_device(): pl.pallas_call(functools.partial(step_kernel, (n_seg, n_lat, n_z, scale))...  97.9 us

profile of v5, /device:TPU:1, one launch (start us, length us, event | category | flops | bytes accessed | tf_op | source)
XLA Modules:
  0.0 100.6 jit_solution(779432784673569104)
XLA Ops:
  0.6 97.9 %section_step.1 = (bf16[2,64,512]{2,1,0:T(8,128)(2,1)S(1)}, bf16[2,64,512]{2,1,0:T(8,128)(2,1)S(1)}, f32[6,512]{1,0:T(8,128)S(1)}) custom-call(s32[9,64]{1,0:T(8,128)} %bitcast.11, s32[9,64]{1,0:T(8,128)} %bitcast.12, f32[9,3,64]{2,1,0:T(4,128)} %bitcast.9, bf16[2,16,4,512]{3,2,1,0:T(4,128)(2,1)} %in_ref.1, bf16[2,16,4,512]{3,2,1,0:T(4,128)(2,1)} %cot_ref.1, ...), custom_call_target="tpu_custom_call" | custom-call | tf_op jit(solution)/shard_map/section_step/pallas_call | solution.py:844
  98.6 0.7 reshape.15
  99.3 0.6 copy.9
  99.9 0.7 reshape.16

commit v6 on v4

--- a/solution.py
+++ b/solution.py
@@ -134,6 +134,7 @@
     z_s,
     z_r,
     w_sem,
+    tokens,
 ):
     n_seg, n_lat, n_z, scale = sizes
     rows, half, channels = in_ref.shape[1:]
@@ -212,8 +213,10 @@
     def greet(device):
         pl.semaphore_signal(barrier, inc=1, device_id=device, device_id_type=MESH)
 
-    for shift in range(1, n_z):
-        greet(at(lax.rem(z + shift, n_z), member, core, lat))
+    z_next = at(lax.rem(z + 1, n_z), member, core, lat)
+    z_prev = at(lax.rem(z + n_z - 1, n_z), member, core, lat)
+    greet(z_next)
+    greet(z_prev)
     greet(on_ring(ring_next))
     greet(on_ring(ring_prev))
     greet(partner)
@@ -239,7 +242,7 @@
     greet(at(z, member, core, lat, seg_next))
     greet(at(z, member, core, lat, seg_prev))
 
-    met = (n_z - 1) + 3 + 2 + 4 + 2
+    met = 2 + 3 + 2 + 4 + 2
     met = met + jnp.where(has_up, 3, 0) + jnp.where(has_down, 3, 0)
     met = met - jnp.where(matched, 2, 0)
     pl.semaphore_wait(barrier, met)
@@ -312,13 +315,28 @@
 
     regroup(in_ref, raw.at[0], 0)
 
+    rounds = n_z // 2 - 1
+
+    def token(number):
+        if 1 < number <= rounds + 1:
+            for way in range(2):
+                pl.semaphore_wait(tokens.at[way, number - 2], 1)
+        if number <= rounds:
+            for way, neighbour in enumerate((z_next, z_prev)):
+                pl.semaphore_signal(
+                    tokens.at[way, number - 1],
+                    inc=1,
+                    device_id=neighbour,
+                    device_id_type=MESH,
+                )
+
+    token(1)
+
     n_pieces = 2 * BASIS
     part_rows = channels // 8
     orders = (tuple(range(n_pieces)), tuple((k + BASIS) % n_pieces for k in range(n_pieces)))
     sections = (seg_prev, seg_next, seg_far)
     parity = lax.rem(z, 2)
-    z_next = at(lax.rem(z + 1, n_z), member, core, lat)
-    z_prev = at(lax.rem(z + n_z - 1, n_z), member, core, lat)
 
     def piece(weights, k, of_parity, of_core):
         start = (2 * of_parity + of_core) * (channels // 4) + (k % 2) * part_rows
@@ -389,7 +407,7 @@
 
     def finish_near():
         for step in range(n_pieces):
-            for way in range(2):
+            for way in (1, 0):
                 k = orders[way][step]
                 side_landed(way, k)
                 swap_copy(way, k, 1).start()
@@ -402,11 +420,18 @@
                 side_copy(2, k).start()
                 swap_copy(2, k, 0).start()
 
-    def near_landed():
-        for step in range(n_pieces):
-            for way in range(2):
-                for other in range(2):
-                    swap_landed(way, orders[way][step], other)
+    def near_landed(way):
+        for k in orders[way]:
+            for other in range(2):
+                swap_landed(way, k, other)
+
+    def weights_here(section):
+        pl.when(seg_far == section)(finish_far)
+        for way in range(2):
+
+            @pl.when(sections[way] == section)
+            def _():
+                near_landed(way)
 
     def finish_far():
         for k in range(n_pieces):
@@ -605,7 +630,9 @@
     pump_near(0, 4)
     regroup_arrived(in_ref, raw.at[0], 0)
     xp[0, pl.ds(0, own), :] = raw[0].reshape(own, channels)
+    token(2)
     halo_start(xp[0, pl.ds(0, own), :], xp.at[0], 0)
+    token(3)
     regroup(cot_ref, raw.at[1], 1)
     pump_near(4, n_pieces)
     fetch.wait()
@@ -616,23 +643,26 @@
 
     finish_near()
     pump_far()
-    near_landed()
-    pl.when(seg_far == 0)(finish_far)
-
     @pl.when(seg != 0)
     def _():
+        weights_here(0)
         forward(0)
 
     for section in range(1, n_seg):
-        pl.when(seg_far == section)(finish_far)
+        token(section + 3)
+        weights_here(section)
         forward(section)
+    for number in range(n_seg + 3, rounds + 1):
+        token(number)
 
     regroup_arrived(cot_ref, raw.at[1], 1)
     grad[...] = raw[1].reshape(own, channels)
 
-    def open_gate(section):
+    def open_gate(section, then=None):
         gate = (grad[...].astype(F32) * slope[section]).astype(BF16)
         gp[section, pl.ds(0, own), :] = gate
+        if then is not None:
+            then()
         halo_start(gate, gp.at[section], n_seg + section)
 
     def pull(section):
@@ -651,11 +681,10 @@
             open_gate(section)
             pull(section)
 
-    open_gate(seg)
     pair_gate = remote(
         gp.at[seg, pl.ds(0, own), :], gate_other, pair_s.at[1], pair_r.at[1], partner
     )
-    pair_gate.start()
+    open_gate(seg, pair_gate.start)
     pair_spread.wait_recv()
     pair_gate.wait_recv()
 
@@ -718,12 +747,11 @@
                 ring_step(1, way, part, 1 - way)
 
     ring_begin()
-    pull(seg)
-    restore_start(grad, grad_ref, 1)
-
     for part in range(parts):
         for way in range(2):
             ring_step(1, way, part, way)
+    pull(seg)
+    restore_start(grad, grad_ref, 1)
     for step in range(2, steps):
         for half_turn in range(2):
             for part in range(parts):
@@ -746,6 +774,7 @@
     slab = parts * 2 * share
     for to in range(n_z):
         zsend[to] = acc[pl.ds(to, slab, stride=n_z), :].astype(BF16)
+    token(rounds + 1)
     for shift in range(1, n_z):
         z_copy(shift).start()
     total = zsend[z].astype(F32)
@@ -879,6 +908,7 @@
             dma((n_z,)),
             dma((n_z,)),
             dma((4,)),
+            pltpu.SemaphoreType.REGULAR((2, max(n_z // 2 - 1, 1))),
         ],
         compiler_params=pltpu.CompilerParams(
             collective_id=0, has_side_effects=True, vmem_limit_bytes=50331648

time: 100 us -> 95.3 us (0.953)
  Pallas kernels: 97.2 us -> 92.6 us
    pallas_call x1, Pallas kernels: 97.2 us -> 92.6 us  [per_device(): pl.pallas_call(functools.partial(step_kernel, (n_seg, n_lat, n_z, scale))...]
where the time goes in v6:
time: 95.3 us; the launch traced here: 95.2 us
  Pallas kernels  92.6 us (97%)
  local copies, waits for them, and re-layouts  1.99 us (2%)
    pallas_call x1, Pallas kernels, per_device(): pl.pallas_call(functools.partial(step_kernel, (n_seg, n_lat, n_z, scale))...  92.6 us

profile of v6, /device:TPU:1, one launch (start us, length us, event | category | flops | bytes accessed | tf_op | source)
XLA Modules:
  0.0 95.2 jit_solution(12782656614554183369)
XLA Ops:
  0.6 92.6 %section_step.1 = (bf16[2,64,512]{2,1,0:T(8,128)(2,1)S(1)}, bf16[2,64,512]{2,1,0:T(8,128)(2,1)S(1)}, f32[6,512]{1,0:T(8,128)S(1)}) custom-call(s32[9,64]{1,0:T(8,128)} %bitcast.11, s32[9,64]{1,0:T(8,128)} %bitcast.12, f32[9,3,64]{2,1,0:T(4,128)} %bitcast.9, bf16[2,16,4,512]{3,2,1,0:T(4,128)(2,1)} %in_ref.1, bf16[2,16,4,512]{3,2,1,0:T(4,128)(2,1)} %cot_ref.1, ...), custom_call_target="tpu_custom_call" | custom-call | tf_op jit(solution)/shard_map/section_step/pallas_call | solution.py:854
  93.2 0.7 reshape.15
  93.9 0.6 copy.9
  94.5 0.7 reshape.16

commit v7 on v6

--- a/solution.py
+++ b/solution.py
@@ -92,6 +92,7 @@
     basis_ref,
     w_all,
     raw,
+    restored,
     pick,
     xp,
     gp,
@@ -555,9 +556,9 @@
                 def _():
                     halo_copy(buffer, phase, number).wait_send()
 
-    def restore_copy(block, output, which, part, arrives_from):
+    def restore_copy(output, which, part, arrives_from):
         return remote(
-            block.at[pl.ds(part * half_cells, half_cells), :],
+            restored.at[which, part],
             output.at[arrives_from],
             oc_s.at[which, part],
             oc_r.at[which, arrives_from],
@@ -566,26 +567,27 @@
 
     def restore_start(block, output, which):
         for part in range(2):
+            restored[which, part] = block[pl.ds(part * half_cells, half_cells), :].reshape(
+                rows, half, channels
+            )
             there = matched & (core == part)
 
             @pl.when(there)
             def _():
                 pltpu.make_async_copy(
-                    block.at[pl.ds(part * half_cells, half_cells), :],
-                    output.at[member],
-                    oc_r.at[which, member],
+                    restored.at[which, part], output.at[member], oc_r.at[which, member]
                 ).start()
 
             @pl.when(jnp.logical_not(there))
             def _():
-                restore_copy(block, output, which, part, member).start()
-
-    def restore_finish(block, output, which):
+                restore_copy(output, which, part, member).start()
+
+    def restore_finish(output, which):
         for part in range(2):
 
             @pl.when(jnp.logical_not(matched & (core == part)))
             def _():
-                restore_copy(block, output, which, part, member).wait_send()
+                restore_copy(output, which, part, member).wait_send()
 
         for origin in range(2):
             here = matched & (member == origin)
@@ -593,14 +595,12 @@
             @pl.when(here)
             def _():
                 pltpu.make_async_copy(
-                    block.at[pl.ds(0, half_cells), :],
-                    output.at[origin],
-                    oc_r.at[which, origin],
+                    restored.at[which, 0], output.at[origin], oc_r.at[which, origin]
                 ).wait()
 
             @pl.when(jnp.logical_not(here))
             def _():
-                restore_copy(block, output, which, 0, origin).wait_recv()
+                restore_copy(output, which, 0, origin).wait_recv()
 
     pair_spread = remote(spread.at[seg], spread_other, pair_s.at[0], pair_r.at[0], partner)
 
@@ -775,10 +775,11 @@
     for to in range(n_z):
         zsend[to] = acc[pl.ds(to, slab, stride=n_z), :].astype(BF16)
     token(rounds + 1)
-    for shift in range(1, n_z):
+    nearest = sorted(range(1, n_z), key=lambda shift: min(shift, n_z - shift))
+    for shift in reversed(nearest):
         z_copy(shift).start()
     total = zsend[z].astype(F32)
-    for shift in range(1, n_z):
+    for shift in nearest:
         from_z = lax.rem(z + n_z - shift, n_z)
         remote(
             zsend.at[0], zrecv.at[from_z], z_s.at[shift], z_r.at[shift], partner
@@ -803,8 +804,8 @@
     wg_ref[:, :wide] = jnp.where(core == 0, mine, theirs)
     wg_ref[:, wide:] = jnp.where(core == 0, theirs, mine)
 
-    restore_finish(xp.at[seg + 1], out_ref, 0)
-    restore_finish(grad, grad_ref, 1)
+    restore_finish(out_ref, 0)
+    restore_finish(grad_ref, 1)
     regroup_sent(in_ref, raw.at[0], 0)
     regroup_sent(cot_ref, raw.at[1], 1)
     for k in range(n_pieces):
@@ -854,8 +855,8 @@
     section_out, section_grad, weight_grad = pl.pallas_call(
         functools.partial(step_kernel, (n_seg, n_lat, n_z, scale)),
         out_shape=(
-            jax.ShapeDtypeStruct((2, rows * half, channels), BF16),
-            jax.ShapeDtypeStruct((2, rows * half, channels), BF16),
+            jax.ShapeDtypeStruct((2, rows, half, channels), BF16),
+            jax.ShapeDtypeStruct((2, rows, half, channels), BF16),
             jax.ShapeDtypeStruct((share, channels), F32),
         ),
         in_specs=[hbm] * 6,
@@ -865,6 +866,7 @@
             pltpu.VMEM((TAPS, rows * n_lat), jnp.int32),
             pltpu.VMEM((TAPS, BASIS, rows * n_lat), F32),
             pltpu.VMEM((n_seg, BASIS, channels, channels), BF16),
+            pltpu.VMEM((2, 2, rows, half, channels), BF16),
             pltpu.VMEM((2, 2, rows, half, channels), BF16),
             pltpu.VMEM((own, own), BF16),
             pltpu.VMEM((n_seg + 1, spots, channels), BF16),

time: 95.3 us -> 94.8 us (level)
    reshape x2 -> x0, local copies, waits for them, and re-layouts: 1.38 us -> none  [the longest x1 0.69 us: per_device(): section_out.reshape(block)]
    unnamed x1 -> x3, local copies, waits for them, and re-layouts: 0.61 us -> 1.92 us
where the time goes in v7:
time: 94.8 us; the launch traced here: 94.7 us
  Pallas kernels  92.1 us (97%)
  local copies, waits for them, and re-layouts  1.92 us (2%)
    pallas_call x1, Pallas kernels, per_device(): pl.pallas_call(functools.partial(step_kernel, (n_seg, n_lat, n_z, scale))...  92.1 us
    unnamed x3, local copies, waits for them, and re-layouts  1.92 us

profile of v7, /device:TPU:1, one launch (start us, length us, event | category | flops | bytes accessed | tf_op | source)
XLA Modules:
  0.0 94.7 jit_solution(751011054760407705)
XLA Ops:
  0.6 92.1 %section_step.1 = (bf16[2,16,4,512]{3,2,1,0:T(4,128)(2,1)S(1)}, bf16[2,16,4,512]{3,2,1,0:T(4,128)(2,1)S(1)}, f32[6,512]{1,0:T(8,128)S(1)}) custom-call(s32[9,64]{1,0:T(8,128)} %bitcast.15, s32[9,64]{1,0:T(8,128)} %bitcast.16, f32[9,3,64]{2,1,0:T(4,128)} %bitcast.13, bf16[2,16,4,512]{3,2,1,0:T(4,128)(2,1)} %in_ref.1, bf16[2,16,4,512]{3,2,1,0:T(4,128)(2,1)} %cot_ref.1, ...), custom_call_target="tpu_custom_call" | custom-call | tf_op jit(solution)/shard_map/section_step/pallas_call | solution.py:855
  92.8 0.6 copy.9
  93.4 0.7 copy.12
  94.0 0.7 copy.13
